TPU v7x, 32 devices: a whole 2x2x4 slice. The times are simulated.
32 devices in a mesh: reg: 16 (over z, x, core), lev: 2 (over y).
Axes of the slice: x: 2, y: 2, z: 4, core: 2. Of those that a mesh axis runs over, the one named last changes fastest.
Arguments:
- state_now: bfloat16 [24, 1280, 2560], P(None, 'reg', 'lev'), may hold values from -6 to 6
- dep_cell: int32 [8, 1280, 2560], P(None, 'reg', 'lev'), may hold values from 0 to 63, as said below
- weight_code: int32 [8, 1280, 2560], P(None, 'reg', 'lev'), may hold values from 0 to 288, as said below
- wave_speed: float32 [8], replicated, may hold values from 0.05 to 5
Outputs:
- state_next: bfloat16 [24, 1280, 2560], P(None, 'reg', 'lev')
Inputs may be any that keep to these rules, and one draw needn't show every extreme that they name: `dep_cell`: 2 * 4 (a + 4) + b + 4 with whole numbers a and b from -4 to 3; both ends of that range occur for a and for b. `weight_code`: 17 a + b with whole numbers a and b from 0 to 16.
All inputs are finite; a program needn't handle non-finite values.
Results may differ from a plain program's by a relative error of at most 0.0084.
Values may be sent and summed in bfloat16 or wider, within the bound.
A program may use at most 64 MiB of HBM per device.

v0:
```python
import math

import jax
import jax.numpy as jnp
from jax import lax
from jax.sharding import PartitionSpec as P

NLAT = 1280
NLON = 2560
MX = 640
MY = 640
FIELDS = 3
HALO = 4


def padded_2(block, sides, width):
    for axis, dim in sides:
        count = lax.axis_size(axis)
        forward = [(i, i + 1) for i in range(count - 1)]
        forward.append((count - 1, 0))
        backward = [(target, source) for source, target in forward]
        low = lax.ppermute(
            lax.slice_in_dim(block, block.shape[dim] - width, None, axis=dim), axis, forward
        )
        high = lax.ppermute(lax.slice_in_dim(block, 0, width, axis=dim), axis, backward)
        block = jnp.concatenate([low, block, high], axis=dim)
    return block


def wave_table(length, modes, offset, amount):
    position = offset + lax.iota(jnp.int32, amount)
    wavenum = lax.iota(jnp.int32, 2 * modes) % modes
    product = position[:, None] * wavenum[None, :] % length
    angles = product.astype(jnp.float32) * (2.0 * math.pi / length)
    cosine_part = lax.iota(jnp.int32, 2 * modes) < modes
    return jnp.where(cosine_part[None, :], jnp.cos(angles), jnp.sin(angles)).astype(jnp.bfloat16)


def implicit_solve(spectral, xindex, speeds):
    wave_x = xindex % MX
    wave_y = lax.iota(jnp.int32, 2 * MY) % MY
    kx_term = 2.0 * math.pi / NLON * wave_x.astype(jnp.float32)
    ky_term = 2.0 * math.pi / NLAT * wave_y.astype(jnp.float32)
    laplace = kx_term[:, None] ** 2 + ky_term[None, :] ** 2
    inside = wave_x[:, None] * wave_x[:, None] + wave_y[None, :] * wave_y[None, :] < MX * MY
    weight_x = jnp.where(wave_x == 0, 1.0, 2.0)
    weight_y = jnp.where(wave_y == 0, 1.0, 2.0)
    factor = jnp.where(inside, weight_x[:, None] * weight_y[None, :], 0.0).astype(jnp.float32)
    speed_sq = speeds[:, None, None]
    vorticity = spectral[:, 0]
    divergence = spectral[:, 1]
    pressure = spectral[:, 2]
    div_new = (divergence + laplace * pressure) / (1.0 + speed_sq * laplace)
    pres_new = pressure - speed_sq * div_new
    stacked = jnp.stack([vorticity, div_new, pres_new], axis=1)
    return (stacked * factor[None, None]).astype(jnp.bfloat16)


def shift_weights(cell_code, code_index):
    shift_row = cell_code // (2 * HALO) - HALO
    shift_col = cell_code % (2 * HALO) - HALO
    weight_row = (code_index // 17).astype(jnp.float32) / 16.0
    weight_col = (code_index % 17).astype(jnp.float32) / 16.0
    row_weights = []
    col_weights = []
    for offset in range(-HALO, HALO + 1):
        row_weights.append(
            jnp.where(shift_row == offset, 1.0 - weight_row, 0.0)
            + jnp.where(shift_row + 1 == offset, weight_row, 0.0)
        )
        col_weights.append(
            jnp.where(shift_col == offset, 1.0 - weight_col, 0.0)
            + jnp.where(shift_col + 1 == offset, weight_col, 0.0)
        )
    return (row_weights, col_weights)


def interpolate_local(padded, row_weights, col_weights):
    levels, rows_pad, cols_pad = padded.shape
    rows_here = rows_pad - 2 * HALO
    cols_here = cols_pad - 2 * HALO
    blended = jnp.zeros((levels, rows_here, cols_here), jnp.float32)
    for row_step in range(2 * HALO + 1):
        inner = jnp.zeros((levels, rows_here, cols_here), jnp.float32)
        for col_step in range(2 * HALO + 1):
            window = padded[:, row_step : row_step + rows_here, col_step : col_step + cols_here]
            inner = inner + col_weights[col_step] * window.astype(jnp.float32)
        blended = blended + row_weights[row_step] * inner
    return blended.astype(jnp.bfloat16)


def per_device(state_now, dep_cell, weight_code, wave_speed):
    stacked, rows_here, cols_here = state_now.shape
    levels = stacked // FIELDS
    col_first = lax.axis_index("lev") * cols_here
    grouped = state_now.reshape(levels, FIELDS, rows_here, cols_here)
    row_weights, col_weights = shift_weights(dep_cell, weight_code)
    passes = []
    for which_field in range(FIELDS):
        padded = padded_2(grouped[:, which_field], (("reg", 1), ("lev", 2)), HALO)
        passes.append(interpolate_local(padded, row_weights, col_weights))
    upstream = jnp.stack(passes, axis=1).reshape(stacked, rows_here, cols_here)
    lon_table = wave_table(NLON, MX, 0, NLON)
    full_rows = lax.all_to_all(upstream, "lev", split_axis=0, concat_axis=2, tiled=True)
    lon_sum = jnp.einsum("krj,jc->krc", full_rows, lon_table, preferred_element_type=jnp.float32)
    lon_coef = (lon_sum / NLON).astype(jnp.bfloat16)
    lat_table = wave_table(NLAT, MY, 0, NLAT)
    spectral = (
        jnp.einsum(
            "klc,ly->kcy",
            lax.all_to_all(lon_coef, "reg", split_axis=2, concat_axis=1, tiled=True),
            lat_table,
            preferred_element_type=jnp.float32,
        )
        / NLAT
    )
    share = spectral.shape[1]
    xindex = lax.axis_index("reg") * share + lax.iota(jnp.int32, share)
    level_count = spectral.shape[0] // FIELDS
    speeds = lax.dynamic_slice_in_dim(
        wave_speed, lax.axis_index("lev") * level_count, level_count, 0
    )
    solved = implicit_solve(spectral.reshape(level_count, FIELDS, share, 2 * MY), xindex, speeds)
    solved = solved.reshape(level_count * FIELDS, share, 2 * MY)
    back_lat = jnp.einsum(
        "kcy,ly->kcl", solved, lat_table, preferred_element_type=jnp.float32
    ).astype(jnp.bfloat16)
    back_coef = lax.all_to_all(back_lat, "reg", split_axis=2, concat_axis=1, tiled=True)
    own_table = wave_table(NLON, MX, col_first, cols_here)
    return jnp.einsum(
        "kcr,jc->krj",
        lax.all_gather(back_coef, "lev", axis=0, tiled=True),
        own_table,
        preferred_element_type=jnp.float32,
    ).astype(jnp.bfloat16)


def solution(mesh):
    placed = (P(None, "reg", "lev"), P(None, "reg", "lev"), P(None, "reg", "lev"), P())
    return jax.shard_map(
        per_device, mesh=mesh, in_specs=placed, out_specs=P(None, "reg", "lev"), check_vma=False
    )
```

profile of v0, /device:TPU:0, one launch (start us, length us, event | category | flops | bytes accessed | tf_op | source)
XLA Modules:
  0.0 738.9 jit_solution(3293429734263387196)
XLA Ops:
  44.9 75.1 %fusion.69 = bf16[8,1,80,1280]{3,2,0,1:T(8,128)(2,1)} fusion(bf16[8,88,1284]{2,1,0:T(8,128)(2,1)S(1)} %get-tuple-element.12, bf16[8,4,1280]{2,1,0:T(4,128)(2,1)S(1)} %collective-permute-done.1, bf16[8,80,1280]{2,1,0:T(8,128)(2,1)} %copy-done.4, bf16[8,88,1284]{2,1,0:T(8,128)(2,1)S(1)} %get-tuple-element.11, ...), kind=kLoop, calls=%fused_computation.152 | loop fusion | flops 333414400 | bytes 127959040 | tf_op jit(solution)/shard_map/stack | solution.py:102
  120.0 76.8 %fusion.70 = bf16[8,1,80,1280]{3,2,0,1:T(8,128)(2,1)} fusion(bf16[8,88,1284]{2,1,0:T(8,128)(2,1)S(1)} %get-tuple-element.16, bf16[8,4,1280]{2,1,0:T(4,128)(2,1)} %copy-done.8, bf16[8,80,1280]{2,1,0:T(8,128)(2,1)} %copy-done.3, bf16[8,88,1284]{2,1,0:T(8,128)(2,1)S(1)} %get-tuple-element.15, bf16[8,4,1280]{2,1,0:T(4,128)(2,1)} %copy-done.5, ...), kind=kLoop, calls=%fused_computation.153 | loop fusion | flops 333414400 | bytes 127959040 | tf_op jit(solution)/shard_map/stack | solution.py:102
  201.2 75.0 %fusion.71 = bf16[8,1,80,1280]{3,2,0,1:T(8,128)(2,1)} fusion(bf16[8,88,1284]{2,1,0:T(8,128)(2,1)S(1)} %get-tuple-element.20, bf16[8,4,1280]{2,1,0:T(4,128)(2,1)S(1)} %copy-done.7, bf16[8,80,1280]{2,1,0:T(8,128)(2,1)} %copy-done.2, bf16[8,88,1284]{2,1,0:T(8,128)(2,1)S(1)} %get-tuple-element.19, bf16[8,4,1280]{2,1,0:T(4,128)(2,1)S(1)} %collective-permute-done.8, ...), kind=kLoop, calls=%fused_computation.154 | loop fusion | flops 333414400 | bytes 127959040 | tf_op jit(solution)/shard_map/stack | solution.py:102
  281.7 6.3 all-to-all-start
  288.1 47.1 %all-to-all-done = bf16[24,80,1280]{2,1,0:T(8,128)(2,1)} async-done(((bf16[24,80,1280]{2,1,0:T(8,128)(2,1)}), bf16[24,80,1280]{2,1,0:T(8,128)(2,1)}, u32[]{:S(2)}, u32[]{:S(2)}) %all-to-all-start) | async-done | bytes 4915232 | tf_op jit(solution)/shard_map/all_to_all | solution.py:104
  338.0 58.4 %multiply_convert_fusion = bf16[12,80,1280]{2,1,0:T(8,128)(2,1)S(1)} fusion(bf16[12,80,2560]{2,1,0:T(8,128)(2,1)S(1)} %bitcast.85, s32[1280]{0:T(1024)S(1)} %add_select_fusion.7, pred[1280]{0:T(1024)(128)(4,1)S(1)} %iota_compare_fusion), kind=kOutput, calls=%fused_computation.36 | convolution fusion | flops 6329958400 | bytes 7379200 | tf_op jit(solution)/shard_map/krj,jc->krc/dot_general | solution.py:105
  396.4 5.9 copy.17
  402.3 9.9 %reshape.160 = bf16[16,2,38400]{2,1,0:T(2,128)(2,1)} reshape(bf16[1280,12,80]{2,1,0:T(8,128)(2,1)} %bitcast.79) | data formatting | bytes 4915200
  412.2 6.3 all-to-all-start.1
  418.9 46.9 %all-to-all-done.1 = bf16[16,2,38400]{2,1,0:T(2,128)(2,1)S(1)} async-done(((bf16[16,2,38400]{2,1,0:T(2,128)(2,1)}), bf16[16,2,38400]{2,1,0:T(2,128)(2,1)S(1)}, u32[]{:S(2)}, u32[]{:S(2)}) %all-to-all-start.1) | async-done | bytes 2457632 | tf_op jit(solution)/shard_map/all_to_all | solution.py:111
  465.8 9.3 %reshape.161 = bf16[1280,12,80]{2,1,0:T(8,128)(2,1)} reshape(bf16[16,2,38400]{2,1,0:T(2,128)(2,1)S(1)} %all-to-all-done.1) | data formatting | bytes 4915200
  475.1 6.9 copy.25
  482.1 6.1 all_to_all.46
  488.1 30.0 %convolution_multiply_fusion = f32[12,80,1280]{2,1,0:T(8,128)S(1)} fusion(bf16[12,1280,80]{1,2,0:T(8,128)(2,1)S(1)} %all_to_all.46, s32[1280]{0:T(1024)S(1)} %add_select_fusion.7, pred[1280]{0:T(1024)(128)(4,1)S(1)} %iota_compare_fusion), kind=kOutput, calls=%fused_computation.44 | convolution fusion | flops 3164979200 | bytes 7379200 | tf_op jit(solution)/shard_map/klc,ly->kcy/dot_general | solution.py:109
  519.6 30.3 %convolution_convert_fusion.1 = bf16[12,80,1280]{2,1,0:T(8,128)(2,1)S(1)} fusion(bf16[12,80,1280]{2,1,0:T(8,128)(2,1)S(1)} %fusion.23, s32[1280]{0:T(1024)S(1)} %add_select_fusion.7, pred[1280]{0:T(1024)(128)(4,1)S(1)} %iota_compare_fusion), kind=kOutput, calls=%fused_computation.46 | convolution fusion | flops 3164979200 | bytes 4921600 | tf_op jit(solution)/shard_map/kcy,ly->kcl/dot_general | solution.py:125
  549.9 5.7 copy.19
  555.6 8.8 %reshape.162 = bf16[16,2,38400]{2,1,0:T(2,128)(2,1)S(1)} reshape(bf16[1280,12,80]{2,1,0:T(8,128)(2,1)} %bitcast.80) | data formatting | bytes 4915200
  564.4 68.5 %all_to_all.54 = bf16[16,2,38400]{2,1,0:T(2,128)(2,1)} all-to-all(bf16[16,2,38400]{2,1,0:T(2,128)(2,1)S(1)} %reshape.162), channel_id=1, replica_groups=mesh['reg'=16,'lev'=2] {'reg'}, dimensions={0} | all-to-all | bytes 4915200 | tf_op jit(solution)/shard_map/all_to_all | solution.py:128
  633.0 10.7 %reshape.163 = bf16[1280,12,80]{2,1,0:T(8,128)(2,1)} reshape(bf16[16,2,38400]{2,1,0:T(2,128)(2,1)} %all_to_all.54) | data formatting | bytes 4915200
  643.7 6.9 copy.20
  650.6 7.1 all_to_all.50
  657.8 27.7 %fusion.109 = bf16[1280,1280,1]{1,0,2:T(8,128)(2,1)S(1)} fusion(s32[1280]{0:T(1024)S(1)} %iota_add_fusion, s32[1280]{0:T(1024)S(1)} %add_select_fusion.7, pred[1280]{0:T(1024)(128)(4,1)S(1)} %iota_compare_fusion), kind=kLoop, calls=%fused_computation.48.clone.clone.1 | loop fusion | flops 18022400 | bytes 3288320 | tf_op jit(solution)/shard_map/kcr,jc->krj/dot_general | solution.py:130
  685.5 36.1 %all-gather.2.cloned.1.call-done = bf16[24,1280,80]{1,2,0:T(8,128)(2,1)} async-done(((bf16[12,1280,80]{1,2,0:T(8,128)(2,1)}), bf16[24,1280,80]{1,2,0:T(8,128)(2,1)}) %all-gather.2.cloned.1.call-update) | async-done | bytes 4915216 | tf_op jit(solution)/shard_map/all_gather | solution.py:132
  721.7 9.9 %convolution_convert_fusion = bf16[24,80,1280]{2,1,0:T(8,128)(2,1)} fusion(bf16[24,1280,80]{1,2,0:T(8,128)(2,1)} %all-gather.2.cloned.1.call-done, bf16[1280,1280,1]{1,0,2:T(8,128)(2,1)S(1)} %fusion.109), kind=kOutput, calls=%fused_computation.31 | convolution fusion | flops 6293913600 | bytes 13107200 | tf_op jit(solution)/shard_map/kcr,jc->krj/dot_general | solution.py:130
  (73 shorter events, 52.7 us)
Async XLA Ops:
  9.3 20.2 %copy-start.2 = (bf16[8,80,1280]{2,1,0:T(8,128)(2,1)}, bf16[8,80,1280]{2,1,0:T(8,128)(2,1)S(1)}, u32[]{:S(2)}) copy-start(bf16[8,80,1280]{2,1,0:T(8,128)(2,1)S(1)} %get-tuple-element.9) | copy-start | bytes 4915204
  9.3 26.3 %copy-start.4 = (bf16[8,80,1280]{2,1,0:T(8,128)(2,1)}, bf16[8,80,1280]{2,1,0:T(8,128)(2,1)S(1)}, u32[]{:S(2)}) copy-start(bf16[8,80,1280]{2,1,0:T(8,128)(2,1)S(1)} %get-tuple-element.8) | copy-start | bytes 4915204
  9.3 33.2 %copy-start.3 = (bf16[8,80,1280]{2,1,0:T(8,128)(2,1)}, bf16[8,80,1280]{2,1,0:T(8,128)(2,1)S(1)}, u32[]{:S(2)}) copy-start(bf16[8,80,1280]{2,1,0:T(8,128)(2,1)S(1)} %get-tuple-element.10) | copy-start | bytes 4915204
  9.4 10.2 %collective-permute-start = (bf16[8,4,1280]{2,1,0:T(4,128)(2,1)S(1)}, bf16[8,4,1280]{2,1,0:T(4,128)(2,1)S(1)}, u32[]{:S(2)}, u32[]{:S(2)}) collective-permute-start(bf16[8,4,1280]{2,1,0:T(4,128)(2,1)S(1)} %get-tuple-element.23), channel_id=1, source_target_pairs={{0,2},{2,4},{4,6},{6,8},{8,10},{10,12},{12,14},{14,16},{16,18},{18... | collective-permute-start | bytes 245768 | tf_op jit(solution)/shard_map/ppermute | solution.py:22
  9.9 14.2 %collective-permute-start.1 = (bf16[8,4,1280]{2,1,0:T(4,128)(2,1)S(1)}, bf16[8,4,1280]{2,1,0:T(4,128)(2,1)S(1)}, u32[]{:S(2)}, u32[]{:S(2)}) collective-permute-start(bf16[8,4,1280]{2,1,0:T(4,128)(2,1)S(1)} %get-tuple-element.24), channel_id=1, source_target_pairs={{2,0},{4,2},{6,4},{8,6},{10,8},{12,10},{14,12},{16,14},{18,16},{20... | collective-permute-start | bytes 245768 | tf_op jit(solution)/shard_map/ppermute | solution.py:25
  15.0 11.2 %collective-permute-start.4 = (bf16[8,4,1280]{2,1,0:T(4,128)(2,1)S(1)}, bf16[8,4,1280]{2,1,0:T(4,128)(2,1)S(1)}, u32[]{:S(2)}, u32[]{:S(2)}) collective-permute-start(bf16[8,4,1280]{2,1,0:T(4,128)(2,1)S(1)} %get-tuple-element.25), channel_id=1, source_target_pairs={{0,2},{2,4},{4,6},{6,8},{8,10},{10,12},{12,14},{14,16},{16,18},{18... | collective-permute-start | bytes 245768 | tf_op jit(solution)/shard_map/ppermute | solution.py:22
  15.1 11.3 %collective-permute-start.5 = (bf16[8,4,1280]{2,1,0:T(4,128)(2,1)S(1)}, bf16[8,4,1280]{2,1,0:T(4,128)(2,1)S(1)}, u32[]{:S(2)}, u32[]{:S(2)}) collective-permute-start(bf16[8,4,1280]{2,1,0:T(4,128)(2,1)S(1)} %get-tuple-element.26), channel_id=1, source_target_pairs={{2,0},{4,2},{6,4},{8,6},{10,8},{12,10},{14,12},{16,14},{18,16},{20... | collective-permute-start | bytes 245768 | tf_op jit(solution)/shard_map/ppermute | solution.py:25
  19.6 8.9 %collective-permute-start.8 = (bf16[8,4,1280]{2,1,0:T(4,128)(2,1)S(1)}, bf16[8,4,1280]{2,1,0:T(4,128)(2,1)S(1)}, u32[]{:S(2)}, u32[]{:S(2)}) collective-permute-start(bf16[8,4,1280]{2,1,0:T(4,128)(2,1)S(1)} %get-tuple-element.27), channel_id=1, source_target_pairs={{0,2},{2,4},{4,6},{6,8},{8,10},{10,12},{12,14},{14,16},{16,18},{18... | collective-permute-start | bytes 245768 | tf_op jit(solution)/shard_map/ppermute | solution.py:22
  19.6 8.9 %collective-permute-start.9 = (bf16[8,4,1280]{2,1,0:T(4,128)(2,1)S(1)}, bf16[8,4,1280]{2,1,0:T(4,128)(2,1)S(1)}, u32[]{:S(2)}, u32[]{:S(2)}) collective-permute-start(bf16[8,4,1280]{2,1,0:T(4,128)(2,1)S(1)} %get-tuple-element.28), channel_id=1, source_target_pairs={{2,0},{4,2},{6,4},{8,6},{10,8},{12,10},{14,12},{16,14},{18,16},{20... | collective-permute-start | bytes 245768 | tf_op jit(solution)/shard_map/ppermute | solution.py:25
  24.2 7.6 %collective-permute-start.2 = (bf16[8,88,4]{2,1,0:T(8,128)(2,1)S(1)}, bf16[8,88,4]{2,1,0:T(8,128)(2,1)S(1)}, u32[]{:S(2)}, u32[]{:S(2)}) collective-permute-start(bf16[8,88,4]{2,1,0:T(8,128)(2,1)S(1)} %get-tuple-element.13), channel_id=1, source_target_pairs={{0,1},{1,0},{2,3},{3,2},{4,5},{5,4},{6,7},{7,6},{8,9},{9,8},{10,11... | collective-permute-start | bytes 16904 | tf_op jit(solution)/shard_map/ppermute | solution.py:22
  26.2 16.3 %copy-start.5 = (bf16[8,4,1280]{2,1,0:T(4,128)(2,1)}, bf16[8,4,1280]{2,1,0:T(4,128)(2,1)S(1)}, u32[]{:S(2)}) copy-start(bf16[8,4,1280]{2,1,0:T(4,128)(2,1)S(1)} %collective-permute-done.4) | copy-start | bytes 245764
  26.2 9.4 %collective-permute-start.3 = (bf16[8,88,4]{2,1,0:T(8,128)(2,1)S(1)}, bf16[8,88,4]{2,1,0:T(8,128)(2,1)S(1)}, u32[]{:S(2)}, u32[]{:S(2)}) collective-permute-start(bf16[8,88,4]{2,1,0:T(8,128)(2,1)S(1)} %get-tuple-element.14), channel_id=1, source_target_pairs={{1,0},{0,1},{3,2},{2,3},{5,4},{4,5},{7,6},{6,7},{9,8},{8,9},{11,10... | collective-permute-start | bytes 16904 | tf_op jit(solution)/shard_map/ppermute | solution.py:25
  26.3 16.2 %copy-start.8 = (bf16[8,4,1280]{2,1,0:T(4,128)(2,1)}, bf16[8,4,1280]{2,1,0:T(4,128)(2,1)S(1)}, u32[]{:S(2)}) copy-start(bf16[8,4,1280]{2,1,0:T(4,128)(2,1)S(1)} %collective-permute-done.5) | copy-start | bytes 245764
  26.5 13.0 %collective-permute-start.6 = (bf16[8,88,4]{2,1,0:T(8,128)(2,1)S(1)}, bf16[8,88,4]{2,1,0:T(8,128)(2,1)S(1)}, u32[]{:S(2)}, u32[]{:S(2)}) collective-permute-start(bf16[8,88,4]{2,1,0:T(8,128)(2,1)S(1)} %get-tuple-element.17), channel_id=1, source_target_pairs={{0,1},{1,0},{2,3},{3,2},{4,5},{5,4},{6,7},{7,6},{8,9},{9,8},{10,11... | collective-permute-start | bytes 16904 | tf_op jit(solution)/shard_map/ppermute | solution.py:22
  28.5 14.1 %collective-permute-start.7 = (bf16[8,88,4]{2,1,0:T(8,128)(2,1)S(1)}, bf16[8,88,4]{2,1,0:T(8,128)(2,1)S(1)}, u32[]{:S(2)}, u32[]{:S(2)}) collective-permute-start(bf16[8,88,4]{2,1,0:T(8,128)(2,1)S(1)} %get-tuple-element.18), channel_id=1, source_target_pairs={{1,0},{0,1},{3,2},{2,3},{5,4},{4,5},{7,6},{6,7},{9,8},{8,9},{11,10... | collective-permute-start | bytes 16904 | tf_op jit(solution)/shard_map/ppermute | solution.py:25
  28.6 5.1 copy-start.6
  29.5 167.4 %collective-permute-start.10 = (bf16[8,88,4]{2,1,0:T(8,128)(2,1)}, bf16[8,88,4]{2,1,0:T(8,128)(2,1)}, u32[]{:S(2)}, u32[]{:S(2)}) collective-permute-start(bf16[8,88,4]{2,1,0:T(8,128)(2,1)} %get-tuple-element.21), channel_id=1, source_target_pairs={{0,1},{1,0},{2,3},{3,2},{4,5},{5,4},{6,7},{7,6},{8,9},{9,8},{10,11... | collective-permute-start | bytes 16904 | tf_op jit(solution)/shard_map/ppermute | solution.py:22
  31.8 165.1 %collective-permute-start.11 = (bf16[8,88,4]{2,1,0:T(8,128)(2,1)}, bf16[8,88,4]{2,1,0:T(8,128)(2,1)}, u32[]{:S(2)}, u32[]{:S(2)}) collective-permute-start(bf16[8,88,4]{2,1,0:T(8,128)(2,1)} %get-tuple-element.22), channel_id=1, source_target_pairs={{1,0},{0,1},{3,2},{2,3},{5,4},{4,5},{7,6},{6,7},{9,8},{8,9},{11,10... | collective-permute-start | bytes 16904 | tf_op jit(solution)/shard_map/ppermute | solution.py:25
  37.9 6.9 copy-start
  120.0 76.9 %copy-start.7 = (bf16[8,4,1280]{2,1,0:T(4,128)(2,1)S(1)}, bf16[8,4,1280]{2,1,0:T(4,128)(2,1)}, u32[]{:S(2)}) copy-start(bf16[8,4,1280]{2,1,0:T(4,128)(2,1)} %copy-done.6) | copy-start | bytes 245764
  281.7 53.4 %all-to-all-start = ((bf16[24,80,1280]{2,1,0:T(8,128)(2,1)}), bf16[24,80,1280]{2,1,0:T(8,128)(2,1)}, u32[]{:S(2)}, u32[]{:S(2)}) async-start(bf16[24,80,1280]{2,1,0:T(8,128)(2,1)} %bitcast.81), calls=%async_computation | async-start | bytes 9830400 | tf_op jit(solution)/shard_map/all_to_all | solution.py:104
  412.2 6.3 copy-start.9
  412.2 53.7 %all-to-all-start.1 = ((bf16[16,2,38400]{2,1,0:T(2,128)(2,1)}), bf16[16,2,38400]{2,1,0:T(2,128)(2,1)S(1)}, u32[]{:S(2)}, u32[]{:S(2)}) async-start(bf16[16,2,38400]{2,1,0:T(2,128)(2,1)} %reshape.160), calls=%async_computation.1 | async-start | bytes 4915200 | tf_op jit(solution)/shard_map/all_to_all | solution.py:111
  418.5 303.2 %all-gather.2.cloned.1.call-start = ((), (), s32[]{:S(2)}) async-start(), calls=%async_computation.3 | async-start | bytes 7372800 | tf_op jit(solution)/shard_map/all_gather | solution.py:132
  (1 other events, 4.3 us)
Sparse Core Ops, SparseCore 0:
  657.9 63.7 all-gather.1
where the time goes:
time: 747 us; the launch traced here: 739 us
  other arithmetic  269 us (36%)
  waiting for transfers between devices  137 us (18%)
  matrix products  129 us (17%)
  local copies, waits for them, and re-layouts  85.9 us (11%)
  blocking collectives  68.5 us (9%)
  starting transfers between devices  35.2 us (5%)
  between operations  14.2 us (2%)
    another operation x4, other arithmetic, per_device(): upstream = jnp.stack(passes, axis=1).reshape(stacked, rows_here, cols_here)  230 us
    all_to_all x1, blocking collectives, per_device(): lax.all_to_all(back_lat, 'reg', split_axis=2, concat_axis=1, tiled=True)  68.5 us
    dot_general x1, matrix products, per_device(): jnp.einsum('krj,jc->krc', full_rows, lon_table, preferred_element_type=jn...  58.4 us
    all_to_all x1, waiting for transfers between devices, per_device(): lax.all_to_all(upstream, 'lev', split_axis=0, concat_axis=2, tiled=True)  47.1 us
    all_to_all x1, waiting for transfers between devices, per_device(): lax.all_to_all(lon_coef, 'reg', split_axis=2, concat_axis=1, tiled=True)  46.9 us
    unnamed x24, local copies, waits for them, and re-layouts  38.7 us
    all_gather x1, waiting for transfers between devices, per_device(): lax.all_gather(back_coef, 'lev', axis=0, tiled=True)  36.1 us
    dot_general x1, matrix products, per_device(): jnp.einsum('kcy,ly->kcl', solved, lat_table, preferred_element_type=jnp.f...  30.3 us
  transfers between devices with their start and end apart: 15, of which 7 were waited for; matrix products, arithmetic and copies ran while one was open for 25% of the time, Pallas kernels for 0%

commit v1 on v0

--- a/solution.py
+++ b/solution.py
@@ -2,7 +2,11 @@
 
 import jax
 import jax.numpy as jnp
+import ml_dtypes
+import numpy as np
 from jax import lax
+from jax.experimental import pallas as pl
+from jax.experimental.pallas import tpu as pltpu
 from jax.sharding import PartitionSpec as P
 
 NLAT = 1280
@@ -11,6 +15,8 @@
 MY = 640
 FIELDS = 3
 HALO = 4
+LANES = 128
+ROWS = 16
 
 
 def padded_2(block, sides, width):
@@ -135,8 +141,265 @@
     ).astype(jnp.bfloat16)
 
 
+def halo_parts(state):
+    rows_here, cols_here = state.shape[1:]
+    count = lax.axis_size("reg")
+    forward = [(i, (i + 1) % count) for i in range(count)]
+    backward = [(target, source) for source, target in forward]
+    low = lax.ppermute(state[:, rows_here - HALO :], "reg", forward)
+    high = lax.ppermute(state[:, :HALO], "reg", backward)
+    edge = jnp.concatenate([low, high], axis=1)
+    edge = jnp.pad(edge, ((0, 0), (0, ROWS - 2 * HALO), (0, 0)))
+    tall = jnp.concatenate(
+        [
+            jnp.concatenate([part[:, :, :LANES], part[:, :, cols_here - LANES :]], axis=2)
+            for part in (state, edge)
+        ],
+        axis=1,
+    )
+    lane = np.r_[0:HALO, 2 * LANES - HALO : 2 * LANES]
+    pick = jnp.asarray((np.arange(2 * LANES)[:, None] == lane[None, :]), jnp.bfloat16)
+    spot = np.r_[LANES : LANES + HALO, LANES - HALO : LANES]
+    place = jnp.asarray((spot[:, None] == np.arange(2 * LANES)[None, :]), jnp.bfloat16)
+    picked = jnp.einsum(
+        "krl,le->ekr", tall, pick, preferred_element_type=jnp.float32
+    ).astype(jnp.bfloat16)
+    other = lax.ppermute(picked, "lev", [(0, 1), (1, 0)])
+    pads = jnp.einsum(
+        "ekr,el->krl", other, place, preferred_element_type=jnp.float32
+    ).astype(jnp.bfloat16)
+    levels = state.shape[0] // FIELDS
+    return (
+        edge.reshape(levels, FIELDS, ROWS, cols_here),
+        pads.reshape(levels, FIELDS, rows_here + ROWS, 2 * LANES),
+    )
+
+
+def mux_pair(parts, bits):
+    for bit, step in zip(bits, (4, 2, 1)):
+        parts = [jnp.where(bit, parts[i + step], parts[i]) for i in range(len(parts) - step)]
+    return parts
+
+
+def interp_kernel(
+    x_ref, edge_ref, pad_ref, dep_ref, weight_ref, out_ref, shift_ref, dep_t, weight_t, result_t
+):
+    levels, rows_here, cols_here = x_ref.shape
+    chunk = out_ref.shape[2]
+    taps = 2 * HALO + 1
+    wide = chunk + 2 * LANES
+
+    def shifted(block):
+        block = jnp.swapaxes(block.astype(jnp.float32), 0, 1)
+        flat = block.reshape(ROWS * levels, wide)
+        for tap in range(taps):
+            turned = pltpu.roll(flat, (HALO - tap) % wide, axis=1)[:, LANES : LANES + chunk]
+            yield tap, turned.reshape(ROWS, levels, chunk)
+
+    def spread(ref, rows, pad_rows, half):
+        if half == 0:
+            parts = [pad_ref[:, pad_rows, :LANES], ref[:, rows, : chunk + LANES]]
+        else:
+            parts = [ref[:, rows, chunk - LANES :], pad_ref[:, pad_rows, LANES:]]
+        return jnp.concatenate(parts, axis=2)
+
+    for half in range(2):
+
+        @pl.when(pl.program_id(0) == half)
+        def _():
+            @pl.loop(0, rows_here // ROWS)
+            def _(group):
+                start = pl.multiple_of(group * ROWS, ROWS)
+                rows = pl.ds(start, ROWS)
+                for tap, turned in shifted(spread(x_ref, rows, rows, half)):
+                    shift_ref[tap, pl.ds(start + HALO, ROWS)] = turned
+
+            edge_rows = slice(rows_here, rows_here + ROWS)
+            for tap, turned in shifted(spread(edge_ref, slice(0, ROWS), edge_rows, half)):
+                shift_ref[tap, :HALO] = turned[:HALO]
+                shift_ref[tap, rows_here + HALO :] = turned[HALO : 2 * HALO]
+
+    pieces = chunk // LANES
+
+    @pl.loop(0, rows_here // ROWS * pieces)
+    def _(step):
+        start = pl.multiple_of(step // pieces * ROWS, ROWS)
+        cols = pl.ds(pl.multiple_of(step % pieces * LANES, LANES), LANES)
+        dep_t[...] = jnp.swapaxes(dep_ref[:, pl.ds(start, ROWS), cols], 0, 1)
+        weight_t[...] = jnp.swapaxes(weight_ref[:, pl.ds(start, ROWS), cols], 0, 1)
+
+        @pl.loop(0, ROWS, step=2)
+        def _(row0):
+            for sub in range(2):
+                row = row0 + sub
+                cell = dep_t[row]
+                row_bits = [(cell & bit) != 0 for bit in (32, 16, 8)]
+                col_bits = [(cell & bit) != 0 for bit in (4, 2, 1)]
+                low, high = [], []
+                for tap in range(taps):
+                    parts = [shift_ref[tap, start + row + i, :, cols] for i in range(taps)]
+                    near, far = mux_pair(parts, row_bits)
+                    low.append(near)
+                    high.append(far)
+                low = mux_pair(low, col_bits)
+                high = mux_pair(high, col_bits)
+                both = weight_t[row]
+                high_part = (both * 241) >> 12
+                weight_row = high_part.astype(jnp.float32) * (1.0 / 16.0)
+                weight_col = (both - 17 * high_part).astype(jnp.float32) * (1.0 / 16.0)
+                upper = (1.0 - weight_col) * low[0] + weight_col * low[1]
+                lower = (1.0 - weight_col) * high[0] + weight_col * high[1]
+                result_t[row] = (1.0 - weight_row) * upper + weight_row * lower
+
+        done = jnp.swapaxes(result_t[...], 0, 1)
+        out_ref[:, pl.ds(start, ROWS), cols] = done.astype(out_ref.dtype)
+
+
+def interpolate(field, state, edge, pads, dep_cell, weight_code):
+    levels, rows_here, cols_here = dep_cell.shape
+    chunk = cols_here // 2
+    taps = 2 * HALO + 1
+
+    def of_field(array):
+        return pl.BlockSpec((levels, None) + array.shape[2:], lambda h: (0, field, 0, 0))
+
+    by_half = pl.BlockSpec((levels, rows_here, chunk), lambda h: (0, 0, h))
+    return pl.pallas_call(
+        interp_kernel,
+        out_shape=jax.ShapeDtypeStruct((levels, rows_here, cols_here), jnp.bfloat16),
+        grid=(2,),
+        in_specs=[of_field(state), of_field(edge), of_field(pads), by_half, by_half],
+        out_specs=by_half,
+        scratch_shapes=[
+            pltpu.VMEM((taps, rows_here + 2 * HALO, levels, chunk), jnp.float32),
+            pltpu.VMEM((ROWS, levels, LANES), jnp.int32),
+            pltpu.VMEM((ROWS, levels, LANES), jnp.int32),
+            pltpu.VMEM((ROWS, levels, LANES), jnp.float32),
+        ],
+        compiler_params=pltpu.CompilerParams(vmem_limit_bytes=44 << 20),
+        cost_estimate=pl.CostEstimate(
+            flops=30 * 10**9, bytes_accessed=90 * 10**6, transcendentals=0
+        ),
+    )(state, edge, pads, dep_cell, weight_code)
+
+
+def host_waves(length, wavenums, amount):
+    angles = (np.arange(amount)[:, None] * wavenums[None, :] % length) * (2.0 * np.pi / length)
+    both = np.stack([np.cos(angles), np.sin(angles)])
+    return both.astype(np.float32).astype(ml_dtypes.bfloat16).transpose(0, 2, 1)
+
+
+def solve_group(spectral, parity, speed):
+    share = spectral[0].shape[0]
+    wave_x = 2 * lax.iota(jnp.int32, share) + parity
+    wave_y = lax.iota(jnp.int32, 2 * MY) % MY
+    kx_term = 2.0 * math.pi / NLON * wave_x.astype(jnp.float32)
+    ky_term = 2.0 * math.pi / NLAT * wave_y.astype(jnp.float32)
+    laplace = kx_term[:, None] ** 2 + ky_term[None, :] ** 2
+    inside = wave_x[:, None] * wave_x[:, None] + wave_y[None, :] * wave_y[None, :] < MX * MY
+    weight_x = jnp.where(wave_x == 0, 1.0, 2.0)
+    weight_y = jnp.where(wave_y == 0, 1.0, 2.0)
+    factor = jnp.where(inside, weight_x[:, None] * weight_y[None, :], 0.0).astype(jnp.float32)
+    div_new = (spectral[1] + laplace * spectral[2]) / (1.0 + speed * laplace)
+    pres_new = spectral[2] - speed * div_new
+    return [(part * factor).astype(jnp.bfloat16) for part in (spectral[0], div_new, pres_new)]
+
+
+def synth_kernel(rows_ref, other_ref, own_ref, crossed_ref, *refs):
+    out_ref = refs[-1]
+    levels, rows_here, width = out_ref.shape
+    total = 0.0
+    for part_ref, table_ref in ((rows_ref, own_ref), (other_ref, crossed_ref)):
+        for group in range(2):
+            part = part_ref[group * levels : (group + 1) * levels]
+            part = part.reshape(levels * rows_here, part.shape[2])
+            total = total + jnp.dot(
+                part, table_ref[group], preferred_element_type=jnp.float32
+            )
+    out_ref[...] = total.astype(out_ref.dtype).reshape(levels, rows_here, width)
+
+
+def synthesize(field, rows, other, own, crossed, out):
+    groups, rows_here, half = rows.shape
+    levels = groups // 2
+    cols_here = own.shape[2]
+    block = 2 * LANES
+    whole = pl.BlockSpec((groups, rows_here, half), lambda j: (0, 0, 0))
+    table = pl.BlockSpec((2, half, block), lambda j: (0, 0, j))
+    earlier = [] if out is None else [out]
+    return pl.pallas_call(
+        synth_kernel,
+        out_shape=jax.ShapeDtypeStruct((levels, FIELDS, rows_here, cols_here), jnp.bfloat16),
+        grid=(cols_here // block,),
+        in_specs=[whole, whole, table, table] + [pl.BlockSpec(memory_space=pl.ANY)] * len(earlier),
+        out_specs=pl.BlockSpec((levels, None, rows_here, block), lambda j: (0, field, 0, j)),
+        input_output_aliases={4: 0} if earlier else {},
+        compiler_params=pltpu.CompilerParams(vmem_limit_bytes=24 << 20),
+        cost_estimate=pl.CostEstimate(
+            flops=2 * 10**9, bytes_accessed=5 * 10**6, transcendentals=0
+        ),
+    )(rows, other, own, crossed, *earlier)
+
+
+def paired_device(state_now, dep_cell, weight_code, wave_speed):
+    stacked, rows_here, cols_here = state_now.shape
+    levels = stacked // FIELDS
+    swap = [(0, 1), (1, 0)]
+    parity = lax.axis_index("lev")
+    half = MX // 2
+    even = jnp.asarray(host_waves(NLON, 2 * np.arange(half), cols_here))
+    odd = jnp.asarray(host_waves(NLON, 2 * np.arange(half) + 1, cols_here))
+    own = jnp.where(parity == 0, even, -odd)
+    crossed = jnp.where(parity == 0, odd, even)
+    lat = host_waves(NLAT, np.arange(MY), NLAT)
+    lat = jnp.asarray(np.concatenate([lat[0], lat[1]], axis=0).T.copy())
+
+    edge, pads = halo_parts(state_now)
+    grouped = state_now.reshape(levels, FIELDS, rows_here, cols_here)
+    spectral = []
+    last = None
+    for field in range(FIELDS):
+        upstream = interpolate(field, grouped, edge, pads, dep_cell, weight_code)
+
+        def partial_sum(table):
+            return jnp.einsum(
+                "vrj,gcj->gvrc", upstream, table, preferred_element_type=jnp.float32
+            ) * (1.0 / NLON)
+
+        leaving = partial_sum(crossed).astype(jnp.bfloat16)
+        held = [leaving, edge] if last is None else [leaving, edge, last]
+        leaving, edge = lax.optimization_barrier(held)[:2]
+        away = lax.ppermute(leaving, "lev", swap)
+        coef = (partial_sum(own) + away.astype(jnp.float32)).astype(jnp.bfloat16)
+        last = coef
+        coef = coef.reshape(2 * levels, rows_here, half)
+        owned = lax.all_to_all(coef, "reg", split_axis=0, concat_axis=0, tiled=True)
+        spectral.append(
+            jnp.einsum(
+                "lc,ly->cy", owned.reshape(NLAT, half), lat, preferred_element_type=jnp.float32
+            )
+            * (1.0 / NLAT)
+        )
+    speed = lax.dynamic_index_in_dim(wave_speed, lax.axis_index("reg") % levels, 0, keepdims=False)
+    out = None
+    for field, solved in enumerate(solve_group(spectral, parity, speed)):
+        back = jnp.einsum(
+            "ly,cy->lc", lat, solved, preferred_element_type=jnp.float32
+        ).astype(jnp.bfloat16)
+        back = back.reshape(2 * levels, rows_here, half)
+        rows = lax.all_to_all(back, "reg", split_axis=0, concat_axis=0, tiled=True)
+        other = lax.ppermute(rows, "lev", swap)
+        out = synthesize(field, rows, other, own, crossed, out)
+    return out.reshape(stacked, rows_here, cols_here)
+
+
 def solution(mesh):
     placed = (P(None, "reg", "lev"), P(None, "reg", "lev"), P(None, "reg", "lev"), P())
+    paired = mesh.shape["lev"] == 2 and mesh.shape["reg"] == 16
     return jax.shard_map(
-        per_device, mesh=mesh, in_specs=placed, out_specs=P(None, "reg", "lev"), check_vma=False
+        paired_device if paired else per_device,
+        mesh=mesh,
+        in_specs=placed,
+        out_specs=P(None, "reg", "lev"),
+        check_vma=False,
     )

time: 747 us -> 342 us (0.46); the launches traced: 739 us -> 341 us
  other arithmetic: 269 us -> 2.5 us
  Pallas kernels: 0 us -> 114 us
  matrix products: 129 us -> 32.6 us
  blocking collectives: 68.5 us -> 0 us
  local copies, waits for them, and re-layouts: 85.9 us -> 17.8 us
  starting transfers between devices: 35.2 us -> 49.1 us
  between operations: 14.2 us -> 0.4 us
  waiting for transfers between devices: 137 us -> 125 us
    another operation x5 -> x0, other arithmetic: 230 us -> none  [the longest x4 230 us: per_device(): upstream = jnp.stack(passes, axis=1).reshape(stacked, rows_here, cols_here)]
    pallas_call x0 -> x6, Pallas kernels: none -> 114 us  [the longest x3 95.6 us: interpolate(): pl.pallas_call(interp_kernel, out_shape=jax.ShapeDtypeStruct((levels, row...]
    dot_general x4 -> x13, matrix products: 129 us -> 32.6 us  [the longest x6 13.3 us: partial_sum(): jnp.einsum('vrj,gcj->gvrc', upstream, table, preferred_element_type=jnp.f...]
    all_to_all x1 -> x0, blocking collectives: 68.5 us -> none  [per_device(): lax.all_to_all(back_lat, 'reg', split_axis=2, concat_axis=1, tiled=True)]
    ppermute x12 -> x9, waiting for transfers between devices: 6.89 us -> 64.3 us  [the longest x3 35.5 us: paired_device(): other = lax.ppermute(rows, 'lev', swap)]
    all_gather x1 -> x0, waiting for transfers between devices: 36.1 us -> none  [per_device(): lax.all_gather(back_coef, 'lev', axis=0, tiled=True)]
    all_to_all x2 -> x6, waiting for transfers between devices: 94 us -> 61.1 us  [the longest x3 46.5 us: paired_device(): rows = lax.all_to_all(back, 'reg', split_axis=0, concat_axis=0, tiled=True)]
    all_to_all x5 -> x0, local copies, waits for them, and re-layouts: 29.9 us -> none  [the longest x2 14.1 us: per_device(): lax.all_to_all(back_lat, 'reg', split_axis=2, concat_axis=1, tiled=True)]
  transfers between devices with their start and end apart: 15 -> 15, of which waited for: 7 -> 9; matrix products, arithmetic and copies ran while one was open for 25% -> 10% of each run, Pallas kernels for 0% -> 22%
where the time goes in v1:
time: 342 us; the launch traced here: 341 us
  waiting for transfers between devices  125 us (37%)
  Pallas kernels  114 us (33%)
  starting transfers between devices  49.1 us (14%)
  matrix products  32.6 us (10%)
  local copies, waits for them, and re-layouts  17.8 us (5%)
    pallas_call x3, Pallas kernels, interpolate(): pl.pallas_call(interp_kernel, out_shape=jax.ShapeDtypeStruct((levels, row...  95.6 us
    all_to_all x3, waiting for transfers between devices, paired_device(): rows = lax.all_to_all(back, 'reg', split_axis=0, concat_axis=0, tiled=True)  46.5 us
    ppermute x3, waiting for transfers between devices, paired_device(): other = lax.ppermute(rows, 'lev', swap)  35.5 us
    ppermute x3, waiting for transfers between devices, paired_device(): away = lax.ppermute(leaving, 'lev', swap)  24 us
    all_to_all x3, starting transfers between devices, paired_device(): rows = lax.all_to_all(back, 'reg', split_axis=0, concat_axis=0, tiled=True)  19.6 us
    pallas_call x3, Pallas kernels, synthesize(): pl.pallas_call(synth_kernel, out_shape=jax.ShapeDtypeStruct((levels, FIEL...  17.9 us
    all_to_all x3, starting transfers between devices, paired_device(): owned = lax.all_to_all(coef, 'reg', split_axis=0, concat_axis=0, tiled=True)  16.6 us
    all_to_all x3, waiting for transfers between devices, paired_device(): owned = lax.all_to_all(coef, 'reg', split_axis=0, concat_axis=0, tiled=True)  14.6 us
  transfers between devices with their start and end apart: 15, of which 9 were waited for; matrix products, arithmetic and copies ran while one was open for 10% of the time, Pallas kernels for 22%

profile of v1, /device:TPU:0, one launch (start us, length us, event | category | flops | bytes accessed | tf_op | source)
XLA Modules:
  0.0 341.4 jit_solution(6085938395691174493)
XLA Ops:
  1.9 5.0 %collective-permute-start.1 = (bf16[24,4,1280]{2,1,0:T(4,128)(2,1)S(1)}, bf16[24,4,1280]{2,1,0:T(4,128)(2,1)S(1)}, u32[]{:S(2)}, u32[]{:S(2)}) collective-permute-start(bf16[24,4,1280]{2,1,0:T(4,128)(2,1)S(1)} %get-tuple-element.18), channel_id=1, source_target_pairs={{2,0},{4,2},{6,4},{8,6},{10,8},{12,10},{14,12},{16,14},{18,16},{20... | collective-permute-start | bytes 737288 | tf_op jit(solution)/shard_map/ppermute | solution.py:150
  20.1 31.9 %shard_map.91 = bf16[8,80,1280]{2,1,0:T(8,128)(2,1)S(1)} custom-call(bf16[8,3,80,1280]{3,2,1,0:T(8,128)(2,1)} %bitcast.133, bf16[8,3,16,1280]{3,2,1,0:T(8,128)(2,1)S(1)} %bitcast.123, bf16[8,3,96,256]{3,2,1,0:T(8,128)(2,1)S(1)} %bitcast.126, s32[8,80,1280]{2,1,0:T(8,128)S(1)} %copy-done, s32[8,80,1280]{2,1,0:T(8,128)S(1)} %copy-done.2), custom_call_target="tpu_custom_call" | custom-call | flops 30000001024 | bytes 90000000 | tf_op jit(solution)/shard_map/pallas_call | solution.py:267
  55.7 31.8 %shard_map.92 = bf16[8,80,1280]{2,1,0:T(8,128)(2,1)S(1)} custom-call(bf16[8,3,80,1280]{3,2,1,0:T(8,128)(2,1)} %bitcast.134, bf16[8,3,16,1280]{3,2,1,0:T(8,128)(2,1)S(1)} %bitcast.124, bf16[8,3,96,256]{3,2,1,0:T(8,128)(2,1)S(1)} %bitcast.127, s32[8,80,1280]{2,1,0:T(8,128)S(1)} %copy-done, s32[8,80,1280]{2,1,0:T(8,128)S(1)} %copy-done.2), custom_call_target="tpu_custom_call" | custom-call | flops 30000001024 | bytes 90000000 | tf_op jit(solution)/shard_map/pallas_call | solution.py:267
  92.0 4.8 %all-to-all-start.4 = ((bf16[16,80,320]{2,1,0:T(8,128)(2,1)}), bf16[16,80,320]{2,1,0:T(8,128)(2,1)}, u32[]{:S(2)}, u32[]{:S(2)}) async-start(bf16[16,80,320]{2,1,0:T(8,128)(2,1)} %bitcast.30), calls=%async_computation.4 | async-start | bytes 1966080 | tf_op jit(solution)/shard_map/all_to_all | solution.py:376
  101.3 31.9 %shard_map.93 = bf16[8,80,1280]{2,1,0:T(8,128)(2,1)S(1)} custom-call(bf16[8,3,80,1280]{3,2,1,0:T(8,128)(2,1)} %bitcast.135, bf16[8,3,16,1280]{3,2,1,0:T(8,128)(2,1)S(1)} %bitcast.125, bf16[8,3,96,256]{3,2,1,0:T(8,128)(2,1)S(1)} %bitcast.128, s32[8,80,1280]{2,1,0:T(8,128)S(1)} %copy-done.1, s32[8,80,1280]{2,1,0:T(8,128)S(1)} %copy-done.3), custom_call_target="tpu_custom_call" | custom-call | flops 30000001024 | bytes 90000000 | tf_op jit(solution)/shard_map/pallas_call | solution.py:267
  136.9 6.1 %all-to-all-start.1 = ((bf16[16,80,320]{2,1,0:T(8,128)(2,1)}), bf16[16,80,320]{2,1,0:T(8,128)(2,1)}, u32[]{:S(2)}, u32[]{:S(2)}) async-start(bf16[16,80,320]{2,1,0:T(8,128)(2,1)} %bitcast.131), calls=%async_computation.1 | async-start | bytes 1966080 | tf_op jit(solution)/shard_map/all_to_all | solution.py:376
  143.1 3.0 fusion.53
  146.2 24.0 %collective-permute-done.5 = bf16[2,8,80,320]{3,2,1,0:T(8,128)(2,1)S(1)} collective-permute-done((bf16[2,8,80,320]{3,2,1,0:T(8,128)(2,1)S(1)}, bf16[2,8,80,320]{3,2,1,0:T(8,128)(2,1)S(1)}, u32[]{:S(2)}, u32[]{:S(2)}) %collective-permute-start.5) | collective-permute-done | bytes 819232 | tf_op jit(solution)/shard_map/ppermute | solution.py:372
  172.7 5.8 %all-to-all-start = ((bf16[16,80,320]{2,1,0:T(8,128)(2,1)}), bf16[16,80,320]{2,1,0:T(8,128)(2,1)S(1)}, u32[]{:S(2)}, u32[]{:S(2)}) async-start(bf16[16,80,320]{2,1,0:T(8,128)(2,1)} %bitcast.132), calls=%async_computation | async-start | bytes 1966080 | tf_op jit(solution)/shard_map/all_to_all | solution.py:376
  178.5 5.8 %fusion.6 = bf16[1280,320]{0,1:T(8,128)(2,1)S(1)} fusion(bf16[1280,1280]{1,0:T(8,128)(2,1)} %constant.72.clone, bf16[1280,320]{1,0:T(8,128)(2,1)} %bitcast.31, f32[1280]{0:T(1024)S(1)} %fusion.94, f32[320]{0:T(512)S(1)} %fusion.98, s32[1280]{0:T(1024)S(1)} %fusion.93, s32[320]{0:T(512)S(1)} %fusion.97), kind=kOutput, calls=%fused_computation.12 | convolution fusion | flops 2100428800 | bytes 4928000 | tf_op jit(solution)/shard_map/ly,cy->lc/dot_general | solution.py:386
  185.7 14.6 %all-to-all-done = bf16[16,80,320]{2,1,0:T(8,128)(2,1)S(1)} async-done(((bf16[16,80,320]{2,1,0:T(8,128)(2,1)}), bf16[16,80,320]{2,1,0:T(8,128)(2,1)S(1)}, u32[]{:S(2)}, u32[]{:S(2)}) %all-to-all-start) | async-done | bytes 819232 | tf_op jit(solution)/shard_map/all_to_all | solution.py:376
  200.3 6.5 %all-to-all-start.5 = ((bf16[16,80,320]{2,1,0:T(8,128)(2,1)}), bf16[16,80,320]{2,1,0:T(8,128)(2,1)S(1)}, u32[]{:S(2)}, u32[]{:S(2)}) async-start(bf16[16,80,320]{2,1,0:T(8,128)(2,1)} %bitcast.33), calls=%async_computation.5 | async-start | bytes 1966080 | tf_op jit(solution)/shard_map/all_to_all | solution.py:390
  207.6 3.3 convolution_multiply_fusion.2
  210.9 3.3 fusion.2
  218.8 9.9 %all-to-all-done.5.rows_ref = bf16[16,80,320]{2,1,0:T(8,128)(2,1)S(1)} async-done(((bf16[16,80,320]{2,1,0:T(8,128)(2,1)}), bf16[16,80,320]{2,1,0:T(8,128)(2,1)S(1)}, u32[]{:S(2)}, u32[]{:S(2)}) %all-to-all-start.5) | async-done | bytes 819232 | tf_op jit(solution)/shard_map/all_to_all | solution.py:390
  228.7 6.5 %all-to-all-start.2 = ((bf16[16,80,320]{2,1,0:T(8,128)(2,1)}), bf16[16,80,320]{2,1,0:T(8,128)(2,1)S(1)}, u32[]{:S(2)}, u32[]{:S(2)}) async-start(bf16[16,80,320]{2,1,0:T(8,128)(2,1)} %bitcast.27), calls=%async_computation.2 | async-start | bytes 1966080 | tf_op jit(solution)/shard_map/all_to_all | solution.py:390
  235.3 3.8 %fusion.5 = bf16[1280,320]{0,1:T(8,128)(2,1)S(1)} fusion(bf16[1280,1280]{1,0:T(8,128)(2,1)} %constant.72.clone, f32[320,1280]{1,0:T(8,128)} %copy-done.19, f32[1280]{0:T(1024)S(1)} %fusion.94, f32[320]{0:T(512)S(1)} %fusion.98, s32[1280]{0:T(1024)S(1)} %fusion.93, s32[320]{0:T(512)S(1)} %fusion.97), kind=kOutput, calls=%fused_computation.11 | convolution fusion | flops 1051443200 | bytes 5747200 | tf_op jit(solution)/shard_map/ly,cy->lc/dot_general | solution.py:386
  240.3 16.8 %all-to-all-done.2.rows_ref = bf16[16,80,320]{2,1,0:T(8,128)(2,1)S(1)} async-done(((bf16[16,80,320]{2,1,0:T(8,128)(2,1)}), bf16[16,80,320]{2,1,0:T(8,128)(2,1)S(1)}, u32[]{:S(2)}, u32[]{:S(2)}) %all-to-all-start.2) | async-done | bytes 819232 | tf_op jit(solution)/shard_map/all_to_all | solution.py:390
  257.1 6.5 %all-to-all-start.3 = ((bf16[16,80,320]{2,1,0:T(8,128)(2,1)}), bf16[16,80,320]{2,1,0:T(8,128)(2,1)S(1)}, u32[]{:S(2)}, u32[]{:S(2)}) async-start(bf16[16,80,320]{2,1,0:T(8,128)(2,1)} %bitcast.129), calls=%async_computation.3 | async-start | bytes 1966080 | tf_op jit(solution)/shard_map/all_to_all | solution.py:390
  265.8 19.8 %all-to-all-done.3.rows_ref = bf16[16,80,320]{2,1,0:T(8,128)(2,1)S(1)} async-done(((bf16[16,80,320]{2,1,0:T(8,128)(2,1)}), bf16[16,80,320]{2,1,0:T(8,128)(2,1)S(1)}, u32[]{:S(2)}, u32[]{:S(2)}) %all-to-all-start.3) | async-done | bytes 819232 | tf_op jit(solution)/shard_map/all_to_all | solution.py:390
  288.4 6.3 %shard_map.94.refs_0_ = bf16[8,3,80,1280]{3,2,1,0:T(8,128)(2,1)} custom-call(bf16[16,80,320]{2,1,0:T(8,128)(2,1)S(1)} %all-to-all-done.5.rows_ref, bf16[16,80,320]{2,1,0:T(8,128)(2,1)} %collective-permute-done.8.other_ref, bf16[2,320,1280]{2,1,0:T(8,128)(2,1)S(1)} %get-tuple-element.20.own_ref, bf16[2,320,1280]{2,1,0:T(8,128)(2,1)S(1)} %get-tuple-element.19.crossed_ref), custom_call_target="tpu_custom_call" | custom-call | flops 2000000000 | bytes 5000000 | tf_op jit(solution)/shard_map/pallas_call | solution.py:330
  294.8 35.1 %collective-permute-done.7.other_ref = bf16[16,80,320]{2,1,0:T(8,128)(2,1)S(1)} collective-permute-done((bf16[16,80,320]{2,1,0:T(8,128)(2,1)S(1)}, bf16[16,80,320]{2,1,0:T(8,128)(2,1)S(1)}, u32[]{:S(2)}, u32[]{:S(2)}) %collective-permute-start.7) | collective-permute-done | bytes 819232 | tf_op jit(solution)/shard_map/ppermute | solution.py:391
  329.9 5.2 %shard_map.95.refs_0_ = bf16[8,3,80,1280]{3,2,1,0:T(8,128)(2,1)} custom-call(bf16[16,80,320]{2,1,0:T(8,128)(2,1)S(1)} %all-to-all-done.3.rows_ref, bf16[16,80,320]{2,1,0:T(8,128)(2,1)S(1)} %collective-permute-done.7.other_ref, bf16[2,320,1280]{2,1,0:T(8,128)(2,1)S(1)} %get-tuple-element.20.own_ref, ...), custom_call_target="tpu_custom_call", output_to_operand_aliasing={{}: (4, {})} | custom-call | flops 2000000000 | bytes 5000000 | tf_op jit(solution)/shard_map/pallas_call | solution.py:330
  335.1 6.3 %shard_map.96 = bf16[8,3,80,1280]{3,2,1,0:T(8,128)(2,1)} custom-call(bf16[16,80,320]{2,1,0:T(8,128)(2,1)S(1)} %all-to-all-done.2.rows_ref, bf16[16,80,320]{2,1,0:T(8,128)(2,1)} %collective-permute-done.6.other_ref, bf16[2,320,1280]{2,1,0:T(8,128)(2,1)S(1)} %get-tuple-element.20.own_ref, ...), custom_call_target="tpu_custom_call", output_to_operand_aliasing={{}: (4, {})} | custom-call | flops 2000000000 | bytes 5000000 | tf_op jit(solution)/shard_map/pallas_call | solution.py:330
  (80 shorter events, 46.7 us)
Async XLA Ops:
  1.4 9.5 %collective-permute-start = (bf16[24,4,1280]{2,1,0:T(4,128)(2,1)S(1)}, bf16[24,4,1280]{2,1,0:T(4,128)(2,1)S(1)}, u32[]{:S(2)}, u32[]{:S(2)}) collective-permute-start(bf16[24,4,1280]{2,1,0:T(4,128)(2,1)S(1)} %get-tuple-element.17), channel_id=1, source_target_pairs={{0,2},{2,4},{4,6},{6,8},{8,10},{10,12},{12,14},{14,16},{16,18},{18... | collective-permute-start | bytes 737288 | tf_op jit(solution)/shard_map/ppermute | solution.py:149
  1.9 9.3 %copy-start.18 = (bf16[256,8,1]{1,0,2:T(8,128)(2,1)S(1)}, bf16[256,8,1]{1,0,2:T(8,128)(2,1)}, u32[]{:S(2)}) copy-start(bf16[256,8,1]{1,0,2:T(8,128)(2,1)} %constant.78) | copy-start | bytes 12292
  1.9 9.0 %collective-permute-start.1 = (bf16[24,4,1280]{2,1,0:T(4,128)(2,1)S(1)}, bf16[24,4,1280]{2,1,0:T(4,128)(2,1)S(1)}, u32[]{:S(2)}, u32[]{:S(2)}) collective-permute-start(bf16[24,4,1280]{2,1,0:T(4,128)(2,1)S(1)} %get-tuple-element.18), channel_id=1, source_target_pairs={{2,0},{4,2},{6,4},{8,6},{10,8},{12,10},{14,12},{16,14},{18,16},{20... | collective-permute-start | bytes 737288 | tf_op jit(solution)/shard_map/ppermute | solution.py:150
  11.6 4.1 %collective-permute-start.2 = (bf16[8,24,96]{2,0,1:T(8,128)(2,1)S(1)}, bf16[8,24,96]{2,0,1:T(8,128)(2,1)S(1)}, u32[]{:S(2)}, u32[]{:S(2)}) collective-permute-start(bf16[8,24,96]{2,0,1:T(8,128)(2,1)S(1)} %fusion.73), channel_id=1, source_target_pairs={{0,1},{1,0},{2,3},{3,2},{4,5},{5,4},{6,7},{7,6},{8,9},{9,8},{10,11... | collective-permute-start | bytes 110600 | tf_op jit(solution)/shard_map/ppermute | solution.py:167
  20.1 31.9 %copy-start.8 = (bf16[2,320,1280]{2,1,0:T(8,128)(2,1)S(1)}, bf16[2,320,1280]{2,1,0:T(8,128)(2,1)}, u32[]{:S(2)}) copy-start(bf16[2,320,1280]{2,1,0:T(8,128)(2,1)} %constant.70.clone) | copy-start | bytes 4915204
  20.1 31.9 %copy-start.11 = (bf16[2,320,1280]{2,1,0:T(8,128)(2,1)S(1)}, bf16[2,320,1280]{2,1,0:T(8,128)(2,1)}, u32[]{:S(2)}) copy-start(bf16[2,320,1280]{2,1,0:T(8,128)(2,1)} %constant.71.clone) | copy-start | bytes 4915204
  53.6 35.5 %collective-permute-start.3 = (bf16[2,8,80,320]{3,2,1,0:T(8,128)(2,1)S(1)}, bf16[2,8,80,320]{3,2,1,0:T(8,128)(2,1)S(1)}, u32[]{:S(2)}, u32[]{:S(2)}) collective-permute-start(bf16[2,8,80,320]{3,2,1,0:T(8,128)(2,1)S(1)} %fusion.43), channel_id=1, source_target_pairs={{0,1},{1,0},{2,3},{3,2},{4,5},{5,4},{6,7},{7,6},{8,9},{9,8},{10,11... | collective-permute-start | bytes 2457608 | tf_op jit(solution)/shard_map/ppermute | solution.py:372
  92.0 44.9 %all-to-all-start.4 = ((bf16[16,80,320]{2,1,0:T(8,128)(2,1)}), bf16[16,80,320]{2,1,0:T(8,128)(2,1)}, u32[]{:S(2)}, u32[]{:S(2)}) async-start(bf16[16,80,320]{2,1,0:T(8,128)(2,1)} %bitcast.30), calls=%async_computation.4 | async-start | bytes 1966080 | tf_op jit(solution)/shard_map/all_to_all | solution.py:376
  96.8 37.7 %collective-permute-start.4 = (bf16[2,8,80,320]{3,2,1,0:T(8,128)(2,1)S(1)}, bf16[2,8,80,320]{3,2,1,0:T(8,128)(2,1)S(1)}, u32[]{:S(2)}, u32[]{:S(2)}) collective-permute-start(bf16[2,8,80,320]{3,2,1,0:T(8,128)(2,1)S(1)} %fusion.48), channel_id=1, source_target_pairs={{0,1},{1,0},{2,3},{3,2},{4,5},{5,4},{6,7},{7,6},{8,9},{9,8},{10,11... | collective-permute-start | bytes 2457608 | tf_op jit(solution)/shard_map/ppermute | solution.py:372
  101.3 33.1 %copy-start.7 = (bf16[8,80,1280]{2,1,0:T(8,128)(2,1)S(1)}, bf16[8,80,1280]{2,1,0:T(8,128)(2,1)}, u32[]{:S(2)}) copy-start(bf16[8,80,1280]{2,1,0:T(8,128)(2,1)} %copy-done.6) | copy-start | bytes 4915204
  101.3 33.1 %copy-start.9 = (bf16[2,320,1280]{2,1,0:T(8,128)(2,1)S(1)}, bf16[2,320,1280]{2,1,0:T(8,128)(2,1)}, u32[]{:S(2)}) copy-start(bf16[2,320,1280]{2,1,0:T(8,128)(2,1)} %constant.70.clone) | copy-start | bytes 4915204
  101.3 33.1 %copy-start.13 = (bf16[2,320,1280]{2,1,0:T(8,128)(2,1)S(1)}, bf16[2,320,1280]{2,1,0:T(8,128)(2,1)}, u32[]{:S(2)}) copy-start(bf16[2,320,1280]{2,1,0:T(8,128)(2,1)} %constant.77) | copy-start | bytes 4915204
  134.5 8.6 %copy-start.10 = (bf16[2,320,1280]{2,1,0:T(8,128)(2,1)S(1)}, bf16[2,320,1280]{2,1,0:T(8,128)(2,1)}, u32[]{:S(2)}) copy-start(bf16[2,320,1280]{2,1,0:T(8,128)(2,1)} %constant.70.clone) | copy-start | bytes 4915204
  136.9 35.8 %all-to-all-start.1 = ((bf16[16,80,320]{2,1,0:T(8,128)(2,1)}), bf16[16,80,320]{2,1,0:T(8,128)(2,1)}, u32[]{:S(2)}, u32[]{:S(2)}) async-start(bf16[16,80,320]{2,1,0:T(8,128)(2,1)} %bitcast.131), calls=%async_computation.1 | async-start | bytes 1966080 | tf_op jit(solution)/shard_map/all_to_all | solution.py:376
  143.1 27.1 %copy-start.14 = (bf16[2,320,1280]{2,1,0:T(8,128)(2,1)S(1)}, bf16[2,320,1280]{2,1,0:T(8,128)(2,1)}, u32[]{:S(2)}) copy-start(bf16[2,320,1280]{2,1,0:T(8,128)(2,1)} %constant.77) | copy-start | bytes 4915204
  146.1 24.1 %collective-permute-start.5 = (bf16[2,8,80,320]{3,2,1,0:T(8,128)(2,1)S(1)}, bf16[2,8,80,320]{3,2,1,0:T(8,128)(2,1)S(1)}, u32[]{:S(2)}, u32[]{:S(2)}) collective-permute-start(bf16[2,8,80,320]{3,2,1,0:T(8,128)(2,1)S(1)} %fusion.53), channel_id=1, source_target_pairs={{0,1},{1,0},{2,3},{3,2},{4,5},{5,4},{6,7},{7,6},{8,9},{9,8},{10,11... | collective-permute-start | bytes 2457608 | tf_op jit(solution)/shard_map/ppermute | solution.py:372
  172.7 27.6 %all-to-all-start = ((bf16[16,80,320]{2,1,0:T(8,128)(2,1)}), bf16[16,80,320]{2,1,0:T(8,128)(2,1)S(1)}, u32[]{:S(2)}, u32[]{:S(2)}) async-start(bf16[16,80,320]{2,1,0:T(8,128)(2,1)} %bitcast.132), calls=%async_computation | async-start | bytes 1966080 | tf_op jit(solution)/shard_map/all_to_all | solution.py:376
  184.4 22.5 %copy-start.16 = (f32[8]{0:T(128)S(1)}, f32[8]{0:T(128)}, u32[]{:S(2)}) copy-start(f32[8]{0:T(128)} %param.12) | copy-start | bytes 100
  200.3 28.4 %all-to-all-start.5 = ((bf16[16,80,320]{2,1,0:T(8,128)(2,1)}), bf16[16,80,320]{2,1,0:T(8,128)(2,1)S(1)}, u32[]{:S(2)}, u32[]{:S(2)}) async-start(bf16[16,80,320]{2,1,0:T(8,128)(2,1)} %bitcast.33), calls=%async_computation.5 | async-start | bytes 1966080 | tf_op jit(solution)/shard_map/all_to_all | solution.py:390
  228.7 28.4 %all-to-all-start.2 = ((bf16[16,80,320]{2,1,0:T(8,128)(2,1)}), bf16[16,80,320]{2,1,0:T(8,128)(2,1)S(1)}, u32[]{:S(2)}, u32[]{:S(2)}) async-start(bf16[16,80,320]{2,1,0:T(8,128)(2,1)} %bitcast.27), calls=%async_computation.2 | async-start | bytes 1966080 | tf_op jit(solution)/shard_map/all_to_all | solution.py:390
  257.1 28.4 %all-to-all-start.3 = ((bf16[16,80,320]{2,1,0:T(8,128)(2,1)}), bf16[16,80,320]{2,1,0:T(8,128)(2,1)S(1)}, u32[]{:S(2)}, u32[]{:S(2)}) async-start(bf16[16,80,320]{2,1,0:T(8,128)(2,1)} %bitcast.129), calls=%async_computation.3 | async-start | bytes 1966080 | tf_op jit(solution)/shard_map/all_to_all | solution.py:390
  263.7 24.7 %collective-permute-start.8 = (bf16[16,80,320]{2,1,0:T(8,128)(2,1)S(1)}, bf16[16,80,320]{2,1,0:T(8,128)(2,1)}, u32[]{:S(2)}, u32[]{:S(2)}) collective-permute-start(bf16[16,80,320]{2,1,0:T(8,128)(2,1)S(1)} %all-to-all-done.5.rows_ref), channel_id=1, source_target_pairs={{0,1},{1,0},{2,3},{3,2},{4,5},{5,4},{6,7},{7,6},{8,9},{9,8},{10,11... | collective-permute-start | bytes 2457608 | tf_op jit(solution)/shard_map/ppermute | solution.py:391
  264.0 71.1 %collective-permute-start.6 = (bf16[16,80,320]{2,1,0:T(8,128)(2,1)S(1)}, bf16[16,80,320]{2,1,0:T(8,128)(2,1)}, u32[]{:S(2)}, u32[]{:S(2)}) collective-permute-start(bf16[16,80,320]{2,1,0:T(8,128)(2,1)S(1)} %all-to-all-done.2.rows_ref), channel_id=1, source_target_pairs={{0,1},{1,0},{2,3},{3,2},{4,5},{5,4},{6,7},{7,6},{8,9},{9,8},{10,11... | collective-permute-start | bytes 2457608 | tf_op jit(solution)/shard_map/ppermute | solution.py:391
  285.5 44.3 %collective-permute-start.7 = (bf16[16,80,320]{2,1,0:T(8,128)(2,1)S(1)}, bf16[16,80,320]{2,1,0:T(8,128)(2,1)S(1)}, u32[]{:S(2)}, u32[]{:S(2)}) collective-permute-start(bf16[16,80,320]{2,1,0:T(8,128)(2,1)S(1)} %all-to-all-done.3.rows_ref), channel_id=1, source_target_pairs={{0,1},{1,0},{2,3},{3,2},{4,5},{5,4},{6,7},{7,6},{8,9},{9,8},{10,11... | collective-permute-start | bytes 2457608 | tf_op jit(solution)/shard_map/ppermute | solution.py:391
  (11 other events, 27.7 us)

commit v2 on v1

--- a/solution.py
+++ b/solution.py
@@ -185,64 +185,68 @@
     x_ref, edge_ref, pad_ref, dep_ref, weight_ref, out_ref, shift_ref, dep_t, weight_t, result_t
 ):
     levels, rows_here, cols_here = x_ref.shape
-    chunk = out_ref.shape[2]
+    chunk = cols_here // 2
+    lanes = 2 * levels
     taps = 2 * HALO + 1
     wide = chunk + 2 * LANES
 
-    def shifted(block):
-        block = jnp.swapaxes(block.astype(jnp.float32), 0, 1)
-        flat = block.reshape(ROWS * levels, wide)
+    def shifted(ref, rows, pad_rows):
+        left = jnp.concatenate(
+            [pad_ref[:, pad_rows, :LANES], ref[:, rows, : chunk + LANES]], axis=2
+        )
+        right = jnp.concatenate(
+            [ref[:, rows, chunk - LANES :], pad_ref[:, pad_rows, LANES:]], axis=2
+        )
+        block = jnp.concatenate([left, right], axis=0).astype(jnp.float32)
+        block = jnp.swapaxes(block, 0, 1)
+        flat = block.reshape(ROWS * lanes, wide)
         for tap in range(taps):
             turned = pltpu.roll(flat, (HALO - tap) % wide, axis=1)[:, LANES : LANES + chunk]
-            yield tap, turned.reshape(ROWS, levels, chunk)
-
-    def spread(ref, rows, pad_rows, half):
-        if half == 0:
-            parts = [pad_ref[:, pad_rows, :LANES], ref[:, rows, : chunk + LANES]]
-        else:
-            parts = [ref[:, rows, chunk - LANES :], pad_ref[:, pad_rows, LANES:]]
-        return jnp.concatenate(parts, axis=2)
-
-    for half in range(2):
-
-        @pl.when(pl.program_id(0) == half)
-        def _():
-            @pl.loop(0, rows_here // ROWS)
-            def _(group):
-                start = pl.multiple_of(group * ROWS, ROWS)
-                rows = pl.ds(start, ROWS)
-                for tap, turned in shifted(spread(x_ref, rows, rows, half)):
-                    shift_ref[tap, pl.ds(start + HALO, ROWS)] = turned
-
-            edge_rows = slice(rows_here, rows_here + ROWS)
-            for tap, turned in shifted(spread(edge_ref, slice(0, ROWS), edge_rows, half)):
-                shift_ref[tap, :HALO] = turned[:HALO]
-                shift_ref[tap, rows_here + HALO :] = turned[HALO : 2 * HALO]
+            yield tap, turned.astype(jnp.bfloat16).reshape(ROWS, lanes, chunk)
+
+    @pl.loop(0, rows_here // ROWS)
+    def _(group):
+        start = pl.multiple_of(group * ROWS, ROWS)
+        rows = pl.ds(start, ROWS)
+        for tap, turned in shifted(x_ref, rows, rows):
+            shift_ref[tap, pl.ds(start + HALO, ROWS)] = turned
+
+    edge_rows = slice(rows_here, rows_here + ROWS)
+    for tap, turned in shifted(edge_ref, slice(0, ROWS), edge_rows):
+        shift_ref[tap, :HALO] = turned[:HALO]
+        shift_ref[tap, rows_here + HALO :] = turned[HALO : 2 * HALO]
 
     pieces = chunk // LANES
+
+    def both_halves(ref, rows, col):
+        parts = [ref[:, rows, pl.ds(pl.multiple_of(col + h * chunk, LANES), LANES)] for h in range(2)]
+        return jnp.swapaxes(jnp.concatenate(parts, axis=0), 0, 1)
 
     @pl.loop(0, rows_here // ROWS * pieces)
     def _(step):
         start = pl.multiple_of(step // pieces * ROWS, ROWS)
-        cols = pl.ds(pl.multiple_of(step % pieces * LANES, LANES), LANES)
-        dep_t[...] = jnp.swapaxes(dep_ref[:, pl.ds(start, ROWS), cols], 0, 1)
-        weight_t[...] = jnp.swapaxes(weight_ref[:, pl.ds(start, ROWS), cols], 0, 1)
+        col = pl.multiple_of(step % pieces * LANES, LANES)
+        cols = pl.ds(col, LANES)
+        dep_t[...] = both_halves(dep_ref, pl.ds(start, ROWS), col)
+        weight_t[...] = both_halves(weight_ref, pl.ds(start, ROWS), col)
 
         @pl.loop(0, ROWS, step=2)
         def _(row0):
             for sub in range(2):
                 row = row0 + sub
                 cell = dep_t[row]
-                row_bits = [(cell & bit) != 0 for bit in (32, 16, 8)]
-                col_bits = [(cell & bit) != 0 for bit in (4, 2, 1)]
+                masks = [
+                    (cell & bit).astype(jnp.float32).astype(jnp.bfloat16) > 0
+                    for bit in (32, 16, 8, 4, 2, 1)
+                ]
                 low, high = [], []
                 for tap in range(taps):
                     parts = [shift_ref[tap, start + row + i, :, cols] for i in range(taps)]
-                    near, far = mux_pair(parts, row_bits)
+                    near, far = mux_pair(parts, masks[:3])
                     low.append(near)
                     high.append(far)
-                low = mux_pair(low, col_bits)
-                high = mux_pair(high, col_bits)
+                low = [part.astype(jnp.float32) for part in mux_pair(low, masks[3:])]
+                high = [part.astype(jnp.float32) for part in mux_pair(high, masks[3:])]
                 both = weight_t[row]
                 high_part = (both * 241) >> 12
                 weight_row = high_part.astype(jnp.float32) * (1.0 / 16.0)
@@ -251,30 +255,31 @@
                 lower = (1.0 - weight_col) * high[0] + weight_col * high[1]
                 result_t[row] = (1.0 - weight_row) * upper + weight_row * lower
 
-        done = jnp.swapaxes(result_t[...], 0, 1)
-        out_ref[:, pl.ds(start, ROWS), cols] = done.astype(out_ref.dtype)
+        done = jnp.swapaxes(result_t[...], 0, 1).astype(out_ref.dtype)
+        for h in range(2):
+            place = pl.ds(pl.multiple_of(col + h * chunk, LANES), LANES)
+            out_ref[:, pl.ds(start, ROWS), place] = done[h * levels : (h + 1) * levels]
 
 
 def interpolate(field, state, edge, pads, dep_cell, weight_code):
     levels, rows_here, cols_here = dep_cell.shape
-    chunk = cols_here // 2
     taps = 2 * HALO + 1
 
     def of_field(array):
         return pl.BlockSpec((levels, None) + array.shape[2:], lambda h: (0, field, 0, 0))
 
-    by_half = pl.BlockSpec((levels, rows_here, chunk), lambda h: (0, 0, h))
+    whole = pl.BlockSpec((levels, rows_here, cols_here), lambda h: (0, 0, 0))
     return pl.pallas_call(
         interp_kernel,
         out_shape=jax.ShapeDtypeStruct((levels, rows_here, cols_here), jnp.bfloat16),
-        grid=(2,),
-        in_specs=[of_field(state), of_field(edge), of_field(pads), by_half, by_half],
-        out_specs=by_half,
+        grid=(1,),
+        in_specs=[of_field(state), of_field(edge), of_field(pads), whole, whole],
+        out_specs=whole,
         scratch_shapes=[
-            pltpu.VMEM((taps, rows_here + 2 * HALO, levels, chunk), jnp.float32),
-            pltpu.VMEM((ROWS, levels, LANES), jnp.int32),
-            pltpu.VMEM((ROWS, levels, LANES), jnp.int32),
-            pltpu.VMEM((ROWS, levels, LANES), jnp.float32),
+            pltpu.VMEM((taps, rows_here + 2 * HALO, 2 * levels, cols_here // 2), jnp.bfloat16),
+            pltpu.VMEM((ROWS, 2 * levels, LANES), jnp.int32),
+            pltpu.VMEM((ROWS, 2 * levels, LANES), jnp.int32),
+            pltpu.VMEM((ROWS, 2 * levels, LANES), jnp.float32),
         ],
         compiler_params=pltpu.CompilerParams(vmem_limit_bytes=44 << 20),
         cost_estimate=pl.CostEstimate(
@@ -381,14 +386,19 @@
             * (1.0 / NLAT)
         )
     speed = lax.dynamic_index_in_dim(wave_speed, lax.axis_index("reg") % levels, 0, keepdims=False)
-    out = None
+    out, others = None, []
     for field, solved in enumerate(solve_group(spectral, parity, speed)):
         back = jnp.einsum(
             "ly,cy->lc", lat, solved, preferred_element_type=jnp.float32
         ).astype(jnp.bfloat16)
         back = back.reshape(2 * levels, rows_here, half)
+        if field == 2:
+            back = lax.optimization_barrier((back, others[0]))[0]
         rows = lax.all_to_all(back, "reg", split_axis=0, concat_axis=0, tiled=True)
+        if field == 2:
+            rows = lax.optimization_barrier((rows, others[1]))[0]
         other = lax.ppermute(rows, "lev", swap)
+        others.append(other)
         out = synthesize(field, rows, other, own, crossed, out)
     return out.reshape(stacked, rows_here, cols_here)
 

time: 342 us -> 290 us (0.85)
  Pallas kernels: 114 us -> 82.1 us
  waiting for transfers between devices: 125 us -> 102 us
    pallas_call x3, Pallas kernels: 95.6 us -> 65.3 us  [interpolate(): pl.pallas_call(interp_kernel, out_shape=jax.ShapeDtypeStruct((levels, row...]
    all_to_all x3, waiting for transfers between devices: 46.5 us -> 31.6 us  [paired_device(): rows = lax.all_to_all(back, 'reg', split_axis=0, concat_axis=0, tiled=True)]
    ppermute x3, waiting for transfers between devices: 35.5 us -> 27.1 us  [paired_device(): other = lax.ppermute(rows, 'lev', swap)]
    unnamed x40 -> x46, local copies, waits for them, and re-layouts: 10.6 us -> 12.7 us
  transfers between devices with their start and end apart: 15 -> 15, of which waited for: 9 -> 9; matrix products, arithmetic and copies ran while one was open for 10% -> 13% of each run, Pallas kernels for 22% -> 19%
where the time goes in v2:
time: 290 us; the launch traced here: 288 us
  waiting for transfers between devices  102 us (35%)
  Pallas kernels  82.1 us (28%)
  starting transfers between devices  47.1 us (16%)
  matrix products  34 us (12%)
  local copies, waits for them, and re-layouts  20.8 us (7%)
    pallas_call x3, Pallas kernels, interpolate(): pl.pallas_call(interp_kernel, out_shape=jax.ShapeDtypeStruct((levels, row...  65.3 us
    all_to_all x3, waiting for transfers between devices, paired_device(): rows = lax.all_to_all(back, 'reg', split_axis=0, concat_axis=0, tiled=True)  31.6 us
    ppermute x3, waiting for transfers between devices, paired_device(): other = lax.ppermute(rows, 'lev', swap)  27.1 us
    ppermute x3, waiting for transfers between devices, paired_device(): away = lax.ppermute(leaving, 'lev', swap)  24 us
    all_to_all x3, starting transfers between devices, paired_device(): rows = lax.all_to_all(back, 'reg', split_axis=0, concat_axis=0, tiled=True)  18.8 us
    pallas_call x3, Pallas kernels, synthesize(): pl.pallas_call(synth_kernel, out_shape=jax.ShapeDtypeStruct((levels, FIEL...  16.8 us
    all_to_all x3, starting transfers between devices, paired_device(): owned = lax.all_to_all(coef, 'reg', split_axis=0, concat_axis=0, tiled=True)  16.8 us
    all_to_all x3, waiting for transfers between devices, paired_device(): owned = lax.all_to_all(coef, 'reg', split_axis=0, concat_axis=0, tiled=True)  14 us
  transfers between devices with their start and end apart: 15, of which 9 were waited for; matrix products, arithmetic and copies ran while one was open for 13% of the time, Pallas kernels for 19%

profile of v2, /device:TPU:0, one launch (start us, length us, event | category | flops | bytes accessed | tf_op | source)
XLA Modules:
  0.0 288.5 jit_solution(677667381534936412)
XLA Ops:
  1.9 5.0 %collective-permute-start.1 = (bf16[24,4,1280]{2,1,0:T(4,128)(2,1)S(1)}, bf16[24,4,1280]{2,1,0:T(4,128)(2,1)S(1)}, u32[]{:S(2)}, u32[]{:S(2)}) collective-permute-start(bf16[24,4,1280]{2,1,0:T(4,128)(2,1)S(1)} %get-tuple-element.22), channel_id=1, source_target_pairs={{2,0},{4,2},{6,4},{8,6},{10,8},{12,10},{14,12},{16,14},{18,16},{20... | collective-permute-start | bytes 737288 | tf_op jit(solution)/shard_map/ppermute | solution.py:150
  20.1 21.8 %shard_map.91 = bf16[8,80,1280]{2,1,0:T(8,128)(2,1)S(1)} custom-call(bf16[8,3,80,1280]{3,2,1,0:T(8,128)(2,1)} %bitcast.133, bf16[8,3,16,1280]{3,2,1,0:T(8,128)(2,1)S(1)} %bitcast.123, bf16[8,3,96,256]{3,2,1,0:T(8,128)(2,1)S(1)} %bitcast.126, s32[8,80,1280]{2,1,0:T(8,128)S(1)} %copy-done.2, s32[8,80,1280]{2,1,0:T(8,128)S(1)} %copy-done.4), custom_call_target="tpu_custom_call" | custom-call | flops 30000001024 | bytes 90000000 | tf_op jit(solution)/shard_map/pallas_call | solution.py:272
  45.6 21.7 %shard_map.92 = bf16[8,80,1280]{2,1,0:T(8,128)(2,1)S(1)} custom-call(bf16[8,3,80,1280]{3,2,1,0:T(8,128)(2,1)} %bitcast.134, bf16[8,3,16,1280]{3,2,1,0:T(8,128)(2,1)S(1)} %bitcast.124, bf16[8,3,96,256]{3,2,1,0:T(8,128)(2,1)S(1)} %bitcast.127, s32[8,80,1280]{2,1,0:T(8,128)S(1)} %copy-done.2, s32[8,80,1280]{2,1,0:T(8,128)S(1)} %copy-done.4), custom_call_target="tpu_custom_call" | custom-call | flops 30000001024 | bytes 90000000 | tf_op jit(solution)/shard_map/pallas_call | solution.py:272
  71.8 4.7 %all-to-all-start.2 = ((bf16[16,80,320]{2,1,0:T(8,128)(2,1)}), bf16[16,80,320]{2,1,0:T(8,128)(2,1)}, u32[]{:S(2)}, u32[]{:S(2)}) async-start(bf16[16,80,320]{2,1,0:T(8,128)(2,1)} %bitcast.28), calls=%async_computation.2 | async-start | bytes 1966080 | tf_op jit(solution)/shard_map/all_to_all | solution.py:381
  81.1 21.8 %shard_map.93 = bf16[8,80,1280]{2,1,0:T(8,128)(2,1)S(1)} custom-call(bf16[8,3,80,1280]{3,2,1,0:T(8,128)(2,1)} %bitcast.135, bf16[8,3,16,1280]{3,2,1,0:T(8,128)(2,1)S(1)} %bitcast.125, bf16[8,3,96,256]{3,2,1,0:T(8,128)(2,1)S(1)} %bitcast.128, s32[8,80,1280]{2,1,0:T(8,128)S(1)} %copy-done.3, s32[8,80,1280]{2,1,0:T(8,128)S(1)} %copy-done.5), custom_call_target="tpu_custom_call" | custom-call | flops 30000001024 | bytes 90000000 | tf_op jit(solution)/shard_map/pallas_call | solution.py:272
  106.6 6.1 %all-to-all-start.1 = ((bf16[16,80,320]{2,1,0:T(8,128)(2,1)}), bf16[16,80,320]{2,1,0:T(8,128)(2,1)}, u32[]{:S(2)}, u32[]{:S(2)}) async-start(bf16[16,80,320]{2,1,0:T(8,128)(2,1)} %bitcast.132), calls=%async_computation.1 | async-start | bytes 1966080 | tf_op jit(solution)/shard_map/all_to_all | solution.py:381
  112.8 3.0 %fusion.53 = bf16[2,8,80,320]{3,2,1,0:T(8,128)(2,1)S(1)} fusion(bf16[8,80,1280]{2,1,0:T(8,128)(2,1)S(1)} %copy-done.7, bf16[2,320,1280]{2,1,0:T(8,128)(2,1)} %constant.71.clone, bf16[2,320,1280]{2,1,0:T(8,128)(2,1)S(1)} %copy-done.12, pred[]{:T(512)S(6)} %eq.26), kind=kOutput, calls=%fused_computation.55 | convolution fusion | flops 1050214400 | bytes 5734401 | tf_op jit(solution)/shard_map/vrj,gcj->gvrc/dot_general | solution.py:370
  115.9 24.0 %collective-permute-done.5 = bf16[2,8,80,320]{3,2,1,0:T(8,128)(2,1)S(1)} collective-permute-done((bf16[2,8,80,320]{3,2,1,0:T(8,128)(2,1)S(1)}, bf16[2,8,80,320]{3,2,1,0:T(8,128)(2,1)S(1)}, u32[]{:S(2)}, u32[]{:S(2)}) %collective-permute-start.5) | collective-permute-done | bytes 819232 | tf_op jit(solution)/shard_map/ppermute | solution.py:377
  142.4 5.9 %all-to-all-start = ((bf16[16,80,320]{2,1,0:T(8,128)(2,1)}), bf16[16,80,320]{2,1,0:T(8,128)(2,1)S(1)}, u32[]{:S(2)}, u32[]{:S(2)}) async-start(bf16[16,80,320]{2,1,0:T(8,128)(2,1)} %bitcast.131), calls=%async_computation | async-start | bytes 1966080 | tf_op jit(solution)/shard_map/all_to_all | solution.py:381
  149.0 5.8 %fusion.5 = bf16[1280,320]{0,1:T(8,128)(2,1)S(1)} fusion(bf16[1280,1280]{1,0:T(8,128)(2,1)} %constant.72.clone, bf16[1280,320]{1,0:T(8,128)(2,1)} %bitcast.29, f32[1280]{0:T(1024)S(1)} %fusion.94, f32[320]{0:T(512)S(1)} %fusion.98, s32[1280]{0:T(1024)S(1)} %fusion.93, s32[320]{0:T(512)S(1)} %fusion.97), kind=kOutput, calls=%fused_computation.11 | convolution fusion | flops 2100428800 | bytes 4928000 | tf_op jit(solution)/shard_map/ly,cy->lc/dot_general | solution.py:391
  156.1 14.0 %all-to-all-done = bf16[16,80,320]{2,1,0:T(8,128)(2,1)S(1)} async-done(((bf16[16,80,320]{2,1,0:T(8,128)(2,1)}), bf16[16,80,320]{2,1,0:T(8,128)(2,1)S(1)}, u32[]{:S(2)}, u32[]{:S(2)}) %all-to-all-start) | async-done | bytes 819232 | tf_op jit(solution)/shard_map/all_to_all | solution.py:381
  170.2 6.5 %all-to-all-start.3 = ((bf16[16,80,320]{2,1,0:T(8,128)(2,1)}), bf16[16,80,320]{2,1,0:T(8,128)(2,1)S(1)}, u32[]{:S(2)}, u32[]{:S(2)}) async-start(bf16[16,80,320]{2,1,0:T(8,128)(2,1)} %bitcast.31), calls=%async_computation.3 | async-start | bytes 1966080 | tf_op jit(solution)/shard_map/all_to_all | solution.py:397
  176.7 3.3 %convolution_multiply_fusion.2 = f32[320,1280]{1,0:T(8,128)S(1)} fusion(bf16[1280,320]{1,0:T(8,128)(2,1)S(1)} %bitcast.130, bf16[1280,1280]{1,0:T(8,128)(2,1)} %constant.72.clone), kind=kOutput, calls=%fused_computation.2 | convolution fusion | flops 1048985600 | bytes 5734400 | tf_op jit(solution)/shard_map/lc,ly->cy/dot_general | solution.py:383
  181.2 3.3 %fusion.2 = f32[320,1280]{1,0:T(8,128)S(1)} fusion(bf16[1280,320]{1,0:T(8,128)(2,1)} %bitcast.25, bf16[1280,1280]{1,0:T(8,128)(2,1)S(1)} %copy-done.19, f32[320,1280]{1,0:T(8,128)S(1)} %convolution_multiply_fusion.2, f32[1280]{0:T(1024)S(1)} %multiply_multiply_fusion, f32[320]{0:T(512)S(1)} %multiply_multiply_fusion.1, f32[]{:T(128)} %bitcast.23), kind=kOutput, calls=%fused_computation.5 | convolution fusion | flops 1051443200 | bytes 7379204 | tf_op jit(solution)/shard_map/lc,ly->cy/dot_general | solution.py:383
  188.4 10.1 %all-to-all-done.3.rows_ref = bf16[16,80,320]{2,1,0:T(8,128)(2,1)S(1)} async-done(((bf16[16,80,320]{2,1,0:T(8,128)(2,1)}), bf16[16,80,320]{2,1,0:T(8,128)(2,1)S(1)}, u32[]{:S(2)}, u32[]{:S(2)}) %all-to-all-start.3) | async-done | bytes 819232 | tf_op jit(solution)/shard_map/all_to_all | solution.py:397
  198.6 6.5 %all-to-all-start.5 = ((bf16[16,80,320]{2,1,0:T(8,128)(2,1)}), bf16[16,80,320]{2,1,0:T(8,128)(2,1)S(1)}, u32[]{:S(2)}, u32[]{:S(2)}) async-start(bf16[16,80,320]{2,1,0:T(8,128)(2,1)} %bitcast.33), calls=%async_computation.5 | async-start | bytes 1966080 | tf_op jit(solution)/shard_map/all_to_all | solution.py:397
  205.4 5.9 %fusion.4 = bf16[1280,320]{0,1:T(8,128)(2,1)} fusion(bf16[1280,1280]{1,0:T(8,128)(2,1)} %constant.72.clone, f32[320,1280]{1,0:T(8,128)} %copy-done.21, f32[320,1280]{1,0:T(8,128)} %copy-done.22, f32[1280]{0:T(1024)S(1)} %fusion.94, f32[320]{0:T(512)S(1)} %fusion.98, s32[1280]{0:T(1024)S(1)} %fusion.93, s32[320]{0:T(512)S(1)} %fusion.97, f32[]{:T(128)} %bitcast.23), kind=kOutput, calls=%fused_computation.10 | convolution fusion | flops 1052262400 | bytes 7385604 | tf_op jit(solution)/shard_map/ly,cy->lc/dot_general | solution.py:391
  213.5 15.7 %collective-permute-done.6.other_ref = bf16[16,80,320]{2,1,0:T(8,128)(2,1)S(1)} collective-permute-done((bf16[16,80,320]{2,1,0:T(8,128)(2,1)S(1)}, bf16[16,80,320]{2,1,0:T(8,128)(2,1)S(1)}, u32[]{:S(2)}, u32[]{:S(2)}) %collective-permute-start.6) | collective-permute-done | bytes 819232 | tf_op jit(solution)/shard_map/ppermute | solution.py:400
  230.1 5.8 %all-to-all-start.4 = ((bf16[16,80,320]{2,1,0:T(8,128)(2,1)}), bf16[16,80,320]{2,1,0:T(8,128)(2,1)S(1)}, u32[]{:S(2)}, u32[]{:S(2)}) async-start(bf16[16,80,320]{2,1,0:T(8,128)(2,1)} %bitcast.129), calls=%async_computation.4 | async-start | bytes 1966080 | tf_op jit(solution)/shard_map/all_to_all | solution.py:397
  236.2 21.5 %all-to-all-done.4.rows_ref = bf16[16,80,320]{2,1,0:T(8,128)(2,1)S(1)} async-done(((bf16[16,80,320]{2,1,0:T(8,128)(2,1)}), bf16[16,80,320]{2,1,0:T(8,128)(2,1)S(1)}, u32[]{:S(2)}, u32[]{:S(2)}) %all-to-all-start.4) | async-done | bytes 819232 | tf_op jit(solution)/shard_map/all_to_all | solution.py:397
  262.5 5.2 %shard_map.94.refs_0_ = bf16[8,3,80,1280]{3,2,1,0:T(8,128)(2,1)} custom-call(bf16[16,80,320]{2,1,0:T(8,128)(2,1)S(1)} %all-to-all-done.3.rows_ref, bf16[16,80,320]{2,1,0:T(8,128)(2,1)S(1)} %copy-done.1, bf16[2,320,1280]{2,1,0:T(8,128)(2,1)S(1)} %get-tuple-element.24.own_ref, bf16[2,320,1280]{2,1,0:T(8,128)(2,1)S(1)} %get-tuple-element.23.crossed_ref), custom_call_target="tpu_custom_call" | custom-call | flops 2000000000 | bytes 5000000 | tf_op jit(solution)/shard_map/pallas_call | solution.py:335
  267.8 6.3 %shard_map.95.refs_0_ = bf16[8,3,80,1280]{3,2,1,0:T(8,128)(2,1)} custom-call(bf16[16,80,320]{2,1,0:T(8,128)(2,1)S(1)} %all-to-all-done.5.rows_ref, bf16[16,80,320]{2,1,0:T(8,128)(2,1)} %collective-permute-done.7.other_ref, bf16[2,320,1280]{2,1,0:T(8,128)(2,1)S(1)} %get-tuple-element.24.own_ref, ...), custom_call_target="tpu_custom_call", output_to_operand_aliasing={{}: (4, {})} | custom-call | flops 2000000000 | bytes 5000000 | tf_op jit(solution)/shard_map/pallas_call | solution.py:335
  274.1 9.1 %collective-permute-done.8.other_ref = bf16[16,80,320]{2,1,0:T(8,128)(2,1)S(1)} collective-permute-done((bf16[16,80,320]{2,1,0:T(8,128)(2,1)S(1)}, bf16[16,80,320]{2,1,0:T(8,128)(2,1)S(1)}, u32[]{:S(2)}, u32[]{:S(2)}) %collective-permute-start.8) | collective-permute-done | bytes 819232 | tf_op jit(solution)/shard_map/ppermute | solution.py:400
  283.3 5.2 %shard_map.96 = bf16[8,3,80,1280]{3,2,1,0:T(8,128)(2,1)} custom-call(bf16[16,80,320]{2,1,0:T(8,128)(2,1)S(1)} %all-to-all-done.4.rows_ref, bf16[16,80,320]{2,1,0:T(8,128)(2,1)S(1)} %collective-permute-done.8.other_ref, bf16[2,320,1280]{2,1,0:T(8,128)(2,1)S(1)} %get-tuple-element.24.own_ref, ...), custom_call_target="tpu_custom_call", output_to_operand_aliasing={{}: (4, {})} | custom-call | flops 2000000000 | bytes 5000000 | tf_op jit(solution)/shard_map/pallas_call | solution.py:335
  (86 shorter events, 49.5 us)
Async XLA Ops:
  1.4 9.5 %collective-permute-start = (bf16[24,4,1280]{2,1,0:T(4,128)(2,1)S(1)}, bf16[24,4,1280]{2,1,0:T(4,128)(2,1)S(1)}, u32[]{:S(2)}, u32[]{:S(2)}) collective-permute-start(bf16[24,4,1280]{2,1,0:T(4,128)(2,1)S(1)} %get-tuple-element.21), channel_id=1, source_target_pairs={{0,2},{2,4},{4,6},{6,8},{8,10},{10,12},{12,14},{14,16},{16,18},{18... | collective-permute-start | bytes 737288 | tf_op jit(solution)/shard_map/ppermute | solution.py:149
  1.9 9.3 %copy-start.20 = (bf16[256,8,1]{1,0,2:T(8,128)(2,1)S(1)}, bf16[256,8,1]{1,0,2:T(8,128)(2,1)}, u32[]{:S(2)}) copy-start(bf16[256,8,1]{1,0,2:T(8,128)(2,1)} %constant.78) | copy-start | bytes 12292
  1.9 9.0 %collective-permute-start.1 = (bf16[24,4,1280]{2,1,0:T(4,128)(2,1)S(1)}, bf16[24,4,1280]{2,1,0:T(4,128)(2,1)S(1)}, u32[]{:S(2)}, u32[]{:S(2)}) collective-permute-start(bf16[24,4,1280]{2,1,0:T(4,128)(2,1)S(1)} %get-tuple-element.22), channel_id=1, source_target_pairs={{2,0},{4,2},{6,4},{8,6},{10,8},{12,10},{14,12},{16,14},{18,16},{20... | collective-permute-start | bytes 737288 | tf_op jit(solution)/shard_map/ppermute | solution.py:150
  11.6 4.1 %collective-permute-start.2 = (bf16[8,24,96]{2,0,1:T(8,128)(2,1)S(1)}, bf16[8,24,96]{2,0,1:T(8,128)(2,1)S(1)}, u32[]{:S(2)}, u32[]{:S(2)}) collective-permute-start(bf16[8,24,96]{2,0,1:T(8,128)(2,1)S(1)} %fusion.73), channel_id=1, source_target_pairs={{0,1},{1,0},{2,3},{3,2},{4,5},{5,4},{6,7},{7,6},{8,9},{9,8},{10,11... | collective-permute-start | bytes 110600 | tf_op jit(solution)/shard_map/ppermute | solution.py:167
  20.1 21.8 %copy-start.10 = (bf16[2,320,1280]{2,1,0:T(8,128)(2,1)S(1)}, bf16[2,320,1280]{2,1,0:T(8,128)(2,1)}, u32[]{:S(2)}) copy-start(bf16[2,320,1280]{2,1,0:T(8,128)(2,1)} %constant.70.clone) | copy-start | bytes 4915204
  20.1 21.8 %copy-start.13 = (bf16[2,320,1280]{2,1,0:T(8,128)(2,1)S(1)}, bf16[2,320,1280]{2,1,0:T(8,128)(2,1)}, u32[]{:S(2)}) copy-start(bf16[2,320,1280]{2,1,0:T(8,128)(2,1)} %constant.71.clone) | copy-start | bytes 4915204
  43.5 25.4 %collective-permute-start.3 = (bf16[2,8,80,320]{3,2,1,0:T(8,128)(2,1)S(1)}, bf16[2,8,80,320]{3,2,1,0:T(8,128)(2,1)S(1)}, u32[]{:S(2)}, u32[]{:S(2)}) collective-permute-start(bf16[2,8,80,320]{3,2,1,0:T(8,128)(2,1)S(1)} %fusion.43), channel_id=1, source_target_pairs={{0,1},{1,0},{2,3},{3,2},{4,5},{5,4},{6,7},{7,6},{8,9},{9,8},{10,11... | collective-permute-start | bytes 2457608 | tf_op jit(solution)/shard_map/ppermute | solution.py:377
  71.8 34.8 %all-to-all-start.2 = ((bf16[16,80,320]{2,1,0:T(8,128)(2,1)}), bf16[16,80,320]{2,1,0:T(8,128)(2,1)}, u32[]{:S(2)}, u32[]{:S(2)}) async-start(bf16[16,80,320]{2,1,0:T(8,128)(2,1)} %bitcast.28), calls=%async_computation.2 | async-start | bytes 1966080 | tf_op jit(solution)/shard_map/all_to_all | solution.py:381
  76.6 27.6 %collective-permute-start.4 = (bf16[2,8,80,320]{3,2,1,0:T(8,128)(2,1)S(1)}, bf16[2,8,80,320]{3,2,1,0:T(8,128)(2,1)S(1)}, u32[]{:S(2)}, u32[]{:S(2)}) collective-permute-start(bf16[2,8,80,320]{3,2,1,0:T(8,128)(2,1)S(1)} %fusion.48), channel_id=1, source_target_pairs={{0,1},{1,0},{2,3},{3,2},{4,5},{5,4},{6,7},{7,6},{8,9},{9,8},{10,11... | collective-permute-start | bytes 2457608 | tf_op jit(solution)/shard_map/ppermute | solution.py:377
  81.1 23.0 %copy-start.9 = (bf16[8,80,1280]{2,1,0:T(8,128)(2,1)S(1)}, bf16[8,80,1280]{2,1,0:T(8,128)(2,1)}, u32[]{:S(2)}) copy-start(bf16[8,80,1280]{2,1,0:T(8,128)(2,1)} %copy-done.8) | copy-start | bytes 4915204
  81.1 23.0 %copy-start.11 = (bf16[2,320,1280]{2,1,0:T(8,128)(2,1)S(1)}, bf16[2,320,1280]{2,1,0:T(8,128)(2,1)}, u32[]{:S(2)}) copy-start(bf16[2,320,1280]{2,1,0:T(8,128)(2,1)} %constant.70.clone) | copy-start | bytes 4915204
  81.1 23.0 %copy-start.15 = (bf16[2,320,1280]{2,1,0:T(8,128)(2,1)S(1)}, bf16[2,320,1280]{2,1,0:T(8,128)(2,1)}, u32[]{:S(2)}) copy-start(bf16[2,320,1280]{2,1,0:T(8,128)(2,1)} %constant.77) | copy-start | bytes 4915204
  104.2 8.6 %copy-start.12 = (bf16[2,320,1280]{2,1,0:T(8,128)(2,1)S(1)}, bf16[2,320,1280]{2,1,0:T(8,128)(2,1)}, u32[]{:S(2)}) copy-start(bf16[2,320,1280]{2,1,0:T(8,128)(2,1)} %constant.70.clone) | copy-start | bytes 4915204
  106.6 6.2 %copy-start.7 = (bf16[8,80,1280]{2,1,0:T(8,128)(2,1)S(1)}, bf16[8,80,1280]{2,1,0:T(8,128)(2,1)}, u32[]{:S(2)}) copy-start(bf16[8,80,1280]{2,1,0:T(8,128)(2,1)} %copy-done.6) | copy-start | bytes 4915204
  106.6 35.8 %all-to-all-start.1 = ((bf16[16,80,320]{2,1,0:T(8,128)(2,1)}), bf16[16,80,320]{2,1,0:T(8,128)(2,1)}, u32[]{:S(2)}, u32[]{:S(2)}) async-start(bf16[16,80,320]{2,1,0:T(8,128)(2,1)} %bitcast.132), calls=%async_computation.1 | async-start | bytes 1966080 | tf_op jit(solution)/shard_map/all_to_all | solution.py:381
  112.8 27.1 %copy-start.16 = (bf16[2,320,1280]{2,1,0:T(8,128)(2,1)S(1)}, bf16[2,320,1280]{2,1,0:T(8,128)(2,1)}, u32[]{:S(2)}) copy-start(bf16[2,320,1280]{2,1,0:T(8,128)(2,1)} %constant.77) | copy-start | bytes 4915204
  115.8 24.1 %collective-permute-start.5 = (bf16[2,8,80,320]{3,2,1,0:T(8,128)(2,1)S(1)}, bf16[2,8,80,320]{3,2,1,0:T(8,128)(2,1)S(1)}, u32[]{:S(2)}, u32[]{:S(2)}) collective-permute-start(bf16[2,8,80,320]{3,2,1,0:T(8,128)(2,1)S(1)} %fusion.53), channel_id=1, source_target_pairs={{0,1},{1,0},{2,3},{3,2},{4,5},{5,4},{6,7},{7,6},{8,9},{9,8},{10,11... | collective-permute-start | bytes 2457608 | tf_op jit(solution)/shard_map/ppermute | solution.py:377
  142.4 27.8 %all-to-all-start = ((bf16[16,80,320]{2,1,0:T(8,128)(2,1)}), bf16[16,80,320]{2,1,0:T(8,128)(2,1)S(1)}, u32[]{:S(2)}, u32[]{:S(2)}) async-start(bf16[16,80,320]{2,1,0:T(8,128)(2,1)} %bitcast.131), calls=%async_computation | async-start | bytes 1966080 | tf_op jit(solution)/shard_map/all_to_all | solution.py:381
  170.2 28.4 %all-to-all-start.3 = ((bf16[16,80,320]{2,1,0:T(8,128)(2,1)}), bf16[16,80,320]{2,1,0:T(8,128)(2,1)S(1)}, u32[]{:S(2)}, u32[]{:S(2)}) async-start(bf16[16,80,320]{2,1,0:T(8,128)(2,1)} %bitcast.31), calls=%async_computation.3 | async-start | bytes 1966080 | tf_op jit(solution)/shard_map/all_to_all | solution.py:397
  198.6 31.6 %all-to-all-start.5 = ((bf16[16,80,320]{2,1,0:T(8,128)(2,1)}), bf16[16,80,320]{2,1,0:T(8,128)(2,1)S(1)}, u32[]{:S(2)}, u32[]{:S(2)}) async-start(bf16[16,80,320]{2,1,0:T(8,128)(2,1)} %bitcast.33), calls=%async_computation.5 | async-start | bytes 1966080 | tf_op jit(solution)/shard_map/all_to_all | solution.py:397
  205.1 24.1 %collective-permute-start.6 = (bf16[16,80,320]{2,1,0:T(8,128)(2,1)S(1)}, bf16[16,80,320]{2,1,0:T(8,128)(2,1)S(1)}, u32[]{:S(2)}, u32[]{:S(2)}) collective-permute-start(bf16[16,80,320]{2,1,0:T(8,128)(2,1)S(1)} %all-to-all-done.3.rows_ref), channel_id=1, source_target_pairs={{0,1},{1,0},{2,3},{3,2},{4,5},{5,4},{6,7},{7,6},{8,9},{9,8},{10,11... | collective-permute-start | bytes 2457608 | tf_op jit(solution)/shard_map/ppermute | solution.py:400
  230.1 27.6 %all-to-all-start.4 = ((bf16[16,80,320]{2,1,0:T(8,128)(2,1)}), bf16[16,80,320]{2,1,0:T(8,128)(2,1)S(1)}, u32[]{:S(2)}, u32[]{:S(2)}) async-start(bf16[16,80,320]{2,1,0:T(8,128)(2,1)} %bitcast.129), calls=%async_computation.4 | async-start | bytes 1966080 | tf_op jit(solution)/shard_map/all_to_all | solution.py:397
  235.9 24.2 %collective-permute-start.7 = (bf16[16,80,320]{2,1,0:T(8,128)(2,1)S(1)}, bf16[16,80,320]{2,1,0:T(8,128)(2,1)}, u32[]{:S(2)}, u32[]{:S(2)}) collective-permute-start(bf16[16,80,320]{2,1,0:T(8,128)(2,1)S(1)} %all-to-all-done.5.rows_ref), channel_id=1, source_target_pairs={{0,1},{1,0},{2,3},{3,2},{4,5},{5,4},{6,7},{7,6},{8,9},{9,8},{10,11... | collective-permute-start | bytes 2457608 | tf_op jit(solution)/shard_map/ppermute | solution.py:400
  260.1 23.2 %collective-permute-start.8 = (bf16[16,80,320]{2,1,0:T(8,128)(2,1)S(1)}, bf16[16,80,320]{2,1,0:T(8,128)(2,1)S(1)}, u32[]{:S(2)}, u32[]{:S(2)}) collective-permute-start(bf16[16,80,320]{2,1,0:T(8,128)(2,1)S(1)} %all-to-all-done.4.rows_ref), channel_id=1, source_target_pairs={{0,1},{1,0},{2,3},{3,2},{4,5},{5,4},{6,7},{7,6},{8,9},{9,8},{10,11... | collective-permute-start | bytes 2457608 | tf_op jit(solution)/shard_map/ppermute | solution.py:400
  (14 other events, 35.5 us)

commit v3 on v2

--- a/solution.py
+++ b/solution.py
@@ -361,30 +361,36 @@
 
     edge, pads = halo_parts(state_now)
     grouped = state_now.reshape(levels, FIELDS, rows_here, cols_here)
+    def partial_sum(upstream, table):
+        return jnp.einsum(
+            "vrj,gcj->gvrc", upstream, table, preferred_element_type=jnp.float32
+        ) * (1.0 / NLON)
+
+    def whole_sum(upstream, away):
+        total = partial_sum(upstream, own) + away.astype(jnp.float32)
+        return total.astype(jnp.bfloat16)
+
+    def to_spectral(coef):
+        coef = coef.reshape(2 * levels, rows_here, half)
+        owned = lax.all_to_all(coef, "reg", split_axis=0, concat_axis=0, tiled=True)
+        return jnp.einsum(
+            "lc,ly->cy", owned.reshape(NLAT, half), lat, preferred_element_type=jnp.float32
+        ) * (1.0 / NLAT)
+
     spectral = []
-    last = None
+    before = None
     for field in range(FIELDS):
         upstream = interpolate(field, grouped, edge, pads, dep_cell, weight_code)
-
-        def partial_sum(table):
-            return jnp.einsum(
-                "vrj,gcj->gvrc", upstream, table, preferred_element_type=jnp.float32
-            ) * (1.0 / NLON)
-
-        leaving = partial_sum(crossed).astype(jnp.bfloat16)
-        held = [leaving, edge] if last is None else [leaving, edge, last]
-        leaving, edge = lax.optimization_barrier(held)[:2]
-        away = lax.ppermute(leaving, "lev", swap)
-        coef = (partial_sum(own) + away.astype(jnp.float32)).astype(jnp.bfloat16)
-        last = coef
-        coef = coef.reshape(2 * levels, rows_here, half)
-        owned = lax.all_to_all(coef, "reg", split_axis=0, concat_axis=0, tiled=True)
-        spectral.append(
-            jnp.einsum(
-                "lc,ly->cy", owned.reshape(NLAT, half), lat, preferred_element_type=jnp.float32
-            )
-            * (1.0 / NLAT)
-        )
+        leaving = partial_sum(upstream, crossed).astype(jnp.bfloat16)
+        if before is None:
+            leaving, edge = lax.optimization_barrier((leaving, edge))
+        else:
+            leaving, away = lax.optimization_barrier((leaving, before[1]))
+            coef = whole_sum(before[0], away)
+            coef, edge, _ = lax.optimization_barrier((coef, edge, leaving))
+            spectral.append(to_spectral(coef))
+        before = (upstream, lax.ppermute(leaving, "lev", swap))
+    spectral.append(to_spectral(whole_sum(*before)))
     speed = lax.dynamic_index_in_dim(wave_speed, lax.axis_index("reg") % levels, 0, keepdims=False)
     out, others = None, []
     for field, solved in enumerate(solve_group(spectral, parity, speed)):

time: 290 us -> 289 us (level)
  waiting for transfers between devices: 102 us -> 95.6 us
  starting transfers between devices: 47.1 us -> 51.6 us
  other arithmetic: 2.5 us -> 6.29 us
    convert_element_type x0 -> x3, other arithmetic: none -> 3.79 us  [whole_sum(): return total.astype(jnp.bfloat16)]
    ppermute x3, starting transfers between devices: 0.97 us -> 4.24 us  [paired_device(): other = lax.ppermute(rows, 'lev', swap)]
    unnamed x46 -> x42, local copies, waits for them, and re-layouts: 12.7 us -> 11.1 us
  transfers between devices with their start and end apart: 15 -> 15, of which waited for: 9 -> 9; matrix products, arithmetic and copies ran while one was open for 13% -> 14% of each run, Pallas kernels for 19% -> 19%
where the time goes in v3:
time: 289 us; the launch traced here: 288 us
  waiting for transfers between devices  95.6 us (33%)
  Pallas kernels  82.1 us (28%)
  starting transfers between devices  51.6 us (18%)
  matrix products  32.8 us (11%)
  local copies, waits for them, and re-layouts  19.2 us (7%)
  other arithmetic  6.29 us (2%)
    pallas_call x3, Pallas kernels, interpolate(): pl.pallas_call(interp_kernel, out_shape=jax.ShapeDtypeStruct((levels, row...  65.3 us
    all_to_all x3, waiting for transfers between devices, paired_device(): rows = lax.all_to_all(back, 'reg', split_axis=0, concat_axis=0, tiled=True)  30.6 us
    ppermute x3, waiting for transfers between devices, paired_device(): other = lax.ppermute(rows, 'lev', swap)  25 us
    ppermute x3, waiting for transfers between devices, paired_device(): before = (upstream, lax.ppermute(leaving, 'lev', swap))  21.3 us
    all_to_all x3, starting transfers between devices, paired_device(): rows = lax.all_to_all(back, 'reg', split_axis=0, concat_axis=0, tiled=True)  18.8 us
    all_to_all x3, starting transfers between devices, to_spectral(): owned = lax.all_to_all(coef, 'reg', split_axis=0, concat_axis=0, tiled=True)  17.4 us
    pallas_call x3, Pallas kernels, synthesize(): pl.pallas_call(synth_kernel, out_shape=jax.ShapeDtypeStruct((levels, FIEL...  16.8 us
    all_to_all x3, waiting for transfers between devices, to_spectral(): owned = lax.all_to_all(coef, 'reg', split_axis=0, concat_axis=0, tiled=True)  14 us
  transfers between devices with their start and end apart: 15, of which 9 were waited for; matrix products, arithmetic and copies ran while one was open for 14% of the time, Pallas kernels for 19%

profile of v3, /device:TPU:0, one launch (start us, length us, event | category | flops | bytes accessed | tf_op | source)
XLA Modules:
  0.0 288.0 jit_solution(11052201007401422853)
XLA Ops:
  1.9 5.0 %collective-permute-start.1 = (bf16[24,4,1280]{2,1,0:T(4,128)(2,1)S(1)}, bf16[24,4,1280]{2,1,0:T(4,128)(2,1)S(1)}, u32[]{:S(2)}, u32[]{:S(2)}) collective-permute-start(bf16[24,4,1280]{2,1,0:T(4,128)(2,1)S(1)} %get-tuple-element.30), channel_id=1, source_target_pairs={{2,0},{4,2},{6,4},{8,6},{10,8},{12,10},{14,12},{16,14},{18,16},{20... | collective-permute-start | bytes 737288 | tf_op jit(solution)/shard_map/ppermute | solution.py:150
  20.1 21.8 %shard_map.91 = bf16[8,80,1280]{2,1,0:T(8,128)(2,1)S(1)} custom-call(bf16[8,3,80,1280]{3,2,1,0:T(8,128)(2,1)} %bitcast.119, bf16[8,3,16,1280]{3,2,1,0:T(8,128)(2,1)S(1)} %bitcast.111, bf16[8,3,96,256]{3,2,1,0:T(8,128)(2,1)S(1)} %bitcast.114, s32[8,80,1280]{2,1,0:T(8,128)S(1)} %copy-done.2, s32[8,80,1280]{2,1,0:T(8,128)S(1)} %copy-done.4), custom_call_target="tpu_custom_call" | custom-call | flops 30000001024 | bytes 90000000 | tf_op jit(solution)/shard_map/pallas_call | solution.py:272
  47.1 21.7 %shard_map.92 = bf16[8,80,1280]{2,1,0:T(8,128)(2,1)S(1)} custom-call(bf16[8,3,80,1280]{3,2,1,0:T(8,128)(2,1)} %bitcast.120, bf16[8,3,16,1280]{3,2,1,0:T(8,128)(2,1)S(1)} %bitcast.112, bf16[8,3,96,256]{3,2,1,0:T(8,128)(2,1)S(1)} %bitcast.115, s32[8,80,1280]{2,1,0:T(8,128)S(1)} %copy-done.2, s32[8,80,1280]{2,1,0:T(8,128)S(1)} %copy-done.4), custom_call_target="tpu_custom_call" | custom-call | flops 30000001024 | bytes 90000000 | tf_op jit(solution)/shard_map/pallas_call | solution.py:272
  68.8 2.7 fusion.17
  75.3 5.4 %all-to-all-start.2 = ((bf16[16,80,320]{2,1,0:T(8,128)(2,1)}), bf16[16,80,320]{2,1,0:T(8,128)(2,1)}, u32[]{:S(2)}, u32[]{:S(2)}) async-start(bf16[16,80,320]{2,1,0:T(8,128)(2,1)} %bitcast.28), calls=%async_computation.2 | async-start | bytes 1966080 | tf_op jit(solution)/shard_map/all_to_all | solution.py:375
  84.6 21.8 %shard_map.93 = bf16[8,80,1280]{2,1,0:T(8,128)(2,1)S(1)} custom-call(bf16[8,3,80,1280]{3,2,1,0:T(8,128)(2,1)} %bitcast.121, bf16[8,3,16,1280]{3,2,1,0:T(8,128)(2,1)S(1)} %bitcast.113, bf16[8,3,96,256]{3,2,1,0:T(8,128)(2,1)S(1)} %bitcast.116, s32[8,80,1280]{2,1,0:T(8,128)S(1)} %copy-done.3, s32[8,80,1280]{2,1,0:T(8,128)S(1)} %copy-done.5), custom_call_target="tpu_custom_call" | custom-call | flops 30000001024 | bytes 90000000 | tf_op jit(solution)/shard_map/pallas_call | solution.py:272
  110.2 6.1 %all-to-all-start.1 = ((bf16[16,80,320]{2,1,0:T(8,128)(2,1)}), bf16[16,80,320]{2,1,0:T(8,128)(2,1)}, u32[]{:S(2)}, u32[]{:S(2)}) async-start(bf16[16,80,320]{2,1,0:T(8,128)(2,1)} %bitcast.24), calls=%async_computation.1 | async-start | bytes 1966080 | tf_op jit(solution)/shard_map/all_to_all | solution.py:375
  119.3 21.3 %collective-permute-done.5 = bf16[2,8,80,320]{3,2,1,0:T(8,128)(2,1)S(1)} collective-permute-done((bf16[2,8,80,320]{3,2,1,0:T(8,128)(2,1)}, bf16[2,8,80,320]{3,2,1,0:T(8,128)(2,1)S(1)}, u32[]{:S(2)}, u32[]{:S(2)}) %collective-permute-start.5) | collective-permute-done | bytes 819232 | tf_op jit(solution)/shard_map/ppermute | solution.py:392
  141.9 5.9 %all-to-all-start = ((bf16[16,80,320]{2,1,0:T(8,128)(2,1)}), bf16[16,80,320]{2,1,0:T(8,128)(2,1)S(1)}, u32[]{:S(2)}, u32[]{:S(2)}) async-start(bf16[16,80,320]{2,1,0:T(8,128)(2,1)} %bitcast.20), calls=%async_computation | async-start | bytes 1966080 | tf_op jit(solution)/shard_map/all_to_all | solution.py:375
  148.4 5.9 %fusion.5 = bf16[1280,320]{0,1:T(8,128)(2,1)S(1)} fusion(bf16[1280,1280]{1,0:T(8,128)(2,1)} %constant.72.clone, bf16[1280,320]{1,0:T(8,128)(2,1)} %bitcast.29, f32[1280]{0:T(1024)S(1)} %fusion.90, f32[320]{0:T(512)S(1)} %fusion.94, s32[1280]{0:T(1024)S(1)} %fusion.89, s32[320]{0:T(512)S(1)} %fusion.93), kind=kOutput, calls=%fused_computation.11 | convolution fusion | flops 2100428800 | bytes 4928000 | tf_op jit(solution)/shard_map/ly,cy->lc/dot_general | solution.py:397
  155.7 13.9 %all-to-all-done = bf16[16,80,320]{2,1,0:T(8,128)(2,1)S(1)} async-done(((bf16[16,80,320]{2,1,0:T(8,128)(2,1)}), bf16[16,80,320]{2,1,0:T(8,128)(2,1)S(1)}, u32[]{:S(2)}, u32[]{:S(2)}) %all-to-all-start) | async-done | bytes 819232 | tf_op jit(solution)/shard_map/all_to_all | solution.py:375
  169.6 6.5 %all-to-all-start.3 = ((bf16[16,80,320]{2,1,0:T(8,128)(2,1)}), bf16[16,80,320]{2,1,0:T(8,128)(2,1)S(1)}, u32[]{:S(2)}, u32[]{:S(2)}) async-start(bf16[16,80,320]{2,1,0:T(8,128)(2,1)} %bitcast.31), calls=%async_computation.3 | async-start | bytes 1966080 | tf_op jit(solution)/shard_map/all_to_all | solution.py:403
  176.2 3.3 %convolution_multiply_fusion.2 = f32[320,1280]{1,0:T(8,128)S(1)} fusion(bf16[1280,320]{1,0:T(8,128)(2,1)S(1)} %bitcast.118, bf16[1280,1280]{1,0:T(8,128)(2,1)} %constant.72.clone), kind=kOutput, calls=%fused_computation.2 | convolution fusion | flops 1048985600 | bytes 5734400 | tf_op jit(solution)/shard_map/lc,ly->cy/dot_general | solution.py:376
  180.7 3.3 %fusion.2 = f32[320,1280]{1,0:T(8,128)S(1)} fusion(bf16[1280,320]{1,0:T(8,128)(2,1)} %bitcast.25, bf16[1280,1280]{1,0:T(8,128)(2,1)S(1)} %copy-done.17, f32[320,1280]{1,0:T(8,128)S(1)} %convolution_multiply_fusion.2, f32[1280]{0:T(1024)S(1)} %multiply_multiply_fusion, f32[320]{0:T(512)S(1)} %multiply_multiply_fusion.1, f32[]{:T(128)} %bitcast.22), kind=kOutput, calls=%fused_computation.5 | convolution fusion | flops 1051443200 | bytes 7379204 | tf_op jit(solution)/shard_map/lc,ly->cy/dot_general | solution.py:376
  187.9 10.2 %all-to-all-done.3.rows_ref = bf16[16,80,320]{2,1,0:T(8,128)(2,1)S(1)} async-done(((bf16[16,80,320]{2,1,0:T(8,128)(2,1)}), bf16[16,80,320]{2,1,0:T(8,128)(2,1)S(1)}, u32[]{:S(2)}, u32[]{:S(2)}) %all-to-all-start.3) | async-done | bytes 819232 | tf_op jit(solution)/shard_map/all_to_all | solution.py:403
  198.0 6.5 %all-to-all-start.5 = ((bf16[16,80,320]{2,1,0:T(8,128)(2,1)}), bf16[16,80,320]{2,1,0:T(8,128)(2,1)S(1)}, u32[]{:S(2)}, u32[]{:S(2)}) async-start(bf16[16,80,320]{2,1,0:T(8,128)(2,1)} %bitcast.33), calls=%async_computation.5 | async-start | bytes 1966080 | tf_op jit(solution)/shard_map/all_to_all | solution.py:403
  206.0 5.8 %fusion.4 = bf16[1280,320]{0,1:T(8,128)(2,1)} fusion(bf16[1280,1280]{1,0:T(8,128)(2,1)} %constant.72.clone, f32[320,1280]{1,0:T(8,128)} %copy-done.19, f32[320,1280]{1,0:T(8,128)} %copy-done.20, f32[1280]{0:T(1024)S(1)} %fusion.90, f32[320]{0:T(512)S(1)} %fusion.94, s32[1280]{0:T(1024)S(1)} %fusion.89, s32[320]{0:T(512)S(1)} %fusion.93, f32[]{:T(128)} %bitcast.22), kind=kOutput, calls=%fused_computation.10 | convolution fusion | flops 1052262400 | bytes 7385604 | tf_op jit(solution)/shard_map/ly,cy->lc/dot_general | solution.py:397
  214.0 14.6 %collective-permute-done.6.other_ref = bf16[16,80,320]{2,1,0:T(8,128)(2,1)S(1)} collective-permute-done((bf16[16,80,320]{2,1,0:T(8,128)(2,1)S(1)}, bf16[16,80,320]{2,1,0:T(8,128)(2,1)S(1)}, u32[]{:S(2)}, u32[]{:S(2)}) %collective-permute-start.6) | collective-permute-done | bytes 819232 | tf_op jit(solution)/shard_map/ppermute | solution.py:406
  229.6 5.8 %all-to-all-start.4 = ((bf16[16,80,320]{2,1,0:T(8,128)(2,1)}), bf16[16,80,320]{2,1,0:T(8,128)(2,1)S(1)}, u32[]{:S(2)}, u32[]{:S(2)}) async-start(bf16[16,80,320]{2,1,0:T(8,128)(2,1)} %bitcast.117), calls=%async_computation.4 | async-start | bytes 1966080 | tf_op jit(solution)/shard_map/all_to_all | solution.py:403
  236.8 20.4 %all-to-all-done.4.rows_ref = bf16[16,80,320]{2,1,0:T(8,128)(2,1)S(1)} async-done(((bf16[16,80,320]{2,1,0:T(8,128)(2,1)}), bf16[16,80,320]{2,1,0:T(8,128)(2,1)S(1)}, u32[]{:S(2)}, u32[]{:S(2)}) %all-to-all-start.4) | async-done | bytes 819232 | tf_op jit(solution)/shard_map/all_to_all | solution.py:403
  263.1 5.2 %shard_map.94.refs_0_ = bf16[8,3,80,1280]{3,2,1,0:T(8,128)(2,1)} custom-call(bf16[16,80,320]{2,1,0:T(8,128)(2,1)S(1)} %all-to-all-done.3.rows_ref, bf16[16,80,320]{2,1,0:T(8,128)(2,1)S(1)} %copy-done.1, bf16[2,320,1280]{2,1,0:T(8,128)(2,1)S(1)} %get-tuple-element.32.own_ref, bf16[2,320,1280]{2,1,0:T(8,128)(2,1)S(1)} %get-tuple-element.31.crossed_ref), custom_call_target="tpu_custom_call" | custom-call | flops 2000000000 | bytes 5000000 | tf_op jit(solution)/shard_map/pallas_call | solution.py:335
  268.3 6.3 %shard_map.95.refs_0_ = bf16[8,3,80,1280]{3,2,1,0:T(8,128)(2,1)} custom-call(bf16[16,80,320]{2,1,0:T(8,128)(2,1)S(1)} %all-to-all-done.5.rows_ref, bf16[16,80,320]{2,1,0:T(8,128)(2,1)} %collective-permute-done.7.other_ref, bf16[2,320,1280]{2,1,0:T(8,128)(2,1)S(1)} %get-tuple-element.32.own_ref, ...), custom_call_target="tpu_custom_call", output_to_operand_aliasing={{}: (4, {})} | custom-call | flops 2000000000 | bytes 5000000 | tf_op jit(solution)/shard_map/pallas_call | solution.py:335
  274.7 8.1 %collective-permute-done.8.other_ref = bf16[16,80,320]{2,1,0:T(8,128)(2,1)S(1)} collective-permute-done((bf16[16,80,320]{2,1,0:T(8,128)(2,1)S(1)}, bf16[16,80,320]{2,1,0:T(8,128)(2,1)S(1)}, u32[]{:S(2)}, u32[]{:S(2)}) %collective-permute-start.8) | collective-permute-done | bytes 819232 | tf_op jit(solution)/shard_map/ppermute | solution.py:406
  282.7 5.2 %shard_map.96 = bf16[8,3,80,1280]{3,2,1,0:T(8,128)(2,1)} custom-call(bf16[16,80,320]{2,1,0:T(8,128)(2,1)S(1)} %all-to-all-done.4.rows_ref, bf16[16,80,320]{2,1,0:T(8,128)(2,1)S(1)} %collective-permute-done.8.other_ref, bf16[2,320,1280]{2,1,0:T(8,128)(2,1)S(1)} %get-tuple-element.32.own_ref, ...), custom_call_target="tpu_custom_call", output_to_operand_aliasing={{}: (4, {})} | custom-call | flops 2000000000 | bytes 5000000 | tf_op jit(solution)/shard_map/pallas_call | solution.py:335
  (85 shorter events, 54.6 us)
Async XLA Ops:
  1.4 9.5 %collective-permute-start = (bf16[24,4,1280]{2,1,0:T(4,128)(2,1)S(1)}, bf16[24,4,1280]{2,1,0:T(4,128)(2,1)S(1)}, u32[]{:S(2)}, u32[]{:S(2)}) collective-permute-start(bf16[24,4,1280]{2,1,0:T(4,128)(2,1)S(1)} %get-tuple-element.29), channel_id=1, source_target_pairs={{0,2},{2,4},{4,6},{6,8},{8,10},{10,12},{12,14},{14,16},{16,18},{18... | collective-permute-start | bytes 737288 | tf_op jit(solution)/shard_map/ppermute | solution.py:149
  1.9 9.3 %copy-start.18 = (bf16[256,8,1]{1,0,2:T(8,128)(2,1)S(1)}, bf16[256,8,1]{1,0,2:T(8,128)(2,1)}, u32[]{:S(2)}) copy-start(bf16[256,8,1]{1,0,2:T(8,128)(2,1)} %constant.78) | copy-start | bytes 12292
  1.9 9.0 %collective-permute-start.1 = (bf16[24,4,1280]{2,1,0:T(4,128)(2,1)S(1)}, bf16[24,4,1280]{2,1,0:T(4,128)(2,1)S(1)}, u32[]{:S(2)}, u32[]{:S(2)}) collective-permute-start(bf16[24,4,1280]{2,1,0:T(4,128)(2,1)S(1)} %get-tuple-element.30), channel_id=1, source_target_pairs={{2,0},{4,2},{6,4},{8,6},{10,8},{12,10},{14,12},{16,14},{18,16},{20... | collective-permute-start | bytes 737288 | tf_op jit(solution)/shard_map/ppermute | solution.py:150
  11.6 4.1 %collective-permute-start.2 = (bf16[8,24,96]{2,0,1:T(8,128)(2,1)S(1)}, bf16[8,24,96]{2,0,1:T(8,128)(2,1)S(1)}, u32[]{:S(2)}, u32[]{:S(2)}) collective-permute-start(bf16[8,24,96]{2,0,1:T(8,128)(2,1)S(1)} %fusion.69), channel_id=1, source_target_pairs={{0,1},{1,0},{2,3},{3,2},{4,5},{5,4},{6,7},{7,6},{8,9},{9,8},{10,11... | collective-permute-start | bytes 110600 | tf_op jit(solution)/shard_map/ppermute | solution.py:167
  20.1 21.8 %copy-start.9 = (bf16[2,320,1280]{2,1,0:T(8,128)(2,1)S(1)}, bf16[2,320,1280]{2,1,0:T(8,128)(2,1)}, u32[]{:S(2)}) copy-start(bf16[2,320,1280]{2,1,0:T(8,128)(2,1)} %constant.70.clone) | copy-start | bytes 4915204
  20.1 21.8 %copy-start.12 = (bf16[2,320,1280]{2,1,0:T(8,128)(2,1)S(1)}, bf16[2,320,1280]{2,1,0:T(8,128)(2,1)}, u32[]{:S(2)}) copy-start(bf16[2,320,1280]{2,1,0:T(8,128)(2,1)} %constant.71.clone) | copy-start | bytes 4915204
  45.0 29.1 %collective-permute-start.3 = (bf16[2,8,80,320]{3,2,1,0:T(8,128)(2,1)S(1)}, bf16[2,8,80,320]{3,2,1,0:T(8,128)(2,1)S(1)}, u32[]{:S(2)}, u32[]{:S(2)}) collective-permute-start(bf16[2,8,80,320]{3,2,1,0:T(8,128)(2,1)S(1)} %fusion.43), channel_id=1, source_target_pairs={{0,1},{1,0},{2,3},{3,2},{4,5},{5,4},{6,7},{7,6},{8,9},{9,8},{10,11... | collective-permute-start | bytes 2457608 | tf_op jit(solution)/shard_map/ppermute | solution.py:392
  74.1 34.9 %collective-permute-start.4 = (bf16[2,8,80,320]{3,2,1,0:T(8,128)(2,1)}, bf16[2,8,80,320]{3,2,1,0:T(8,128)(2,1)S(1)}, u32[]{:S(2)}, u32[]{:S(2)}) collective-permute-start(bf16[2,8,80,320]{3,2,1,0:T(8,128)(2,1)} %fusion.48), channel_id=1, source_target_pairs={{0,1},{1,0},{2,3},{3,2},{4,5},{5,4},{6,7},{7,6},{8,9},{9,8},{10,11... | collective-permute-start | bytes 2457608 | tf_op jit(solution)/shard_map/ppermute | solution.py:392
  75.3 34.9 %all-to-all-start.2 = ((bf16[16,80,320]{2,1,0:T(8,128)(2,1)}), bf16[16,80,320]{2,1,0:T(8,128)(2,1)}, u32[]{:S(2)}, u32[]{:S(2)}) async-start(bf16[16,80,320]{2,1,0:T(8,128)(2,1)} %bitcast.28), calls=%async_computation.2 | async-start | bytes 1966080 | tf_op jit(solution)/shard_map/all_to_all | solution.py:375
  84.6 21.8 %copy-start.10 = (bf16[2,320,1280]{2,1,0:T(8,128)(2,1)S(1)}, bf16[2,320,1280]{2,1,0:T(8,128)(2,1)}, u32[]{:S(2)}) copy-start(bf16[2,320,1280]{2,1,0:T(8,128)(2,1)} %constant.70.clone) | copy-start | bytes 4915204
  84.6 21.8 %copy-start.13 = (bf16[2,320,1280]{2,1,0:T(8,128)(2,1)S(1)}, bf16[2,320,1280]{2,1,0:T(8,128)(2,1)}, u32[]{:S(2)}) copy-start(bf16[2,320,1280]{2,1,0:T(8,128)(2,1)} %constant.71.clone) | copy-start | bytes 4915204
  108.9 8.9 %copy-start.11 = (bf16[2,320,1280]{2,1,0:T(8,128)(2,1)S(1)}, bf16[2,320,1280]{2,1,0:T(8,128)(2,1)}, u32[]{:S(2)}) copy-start(bf16[2,320,1280]{2,1,0:T(8,128)(2,1)} %constant.70.clone) | copy-start | bytes 4915204
  110.2 7.6 %copy-start.7 = (bf16[8,80,1280]{2,1,0:T(8,128)(2,1)S(1)}, bf16[8,80,1280]{2,1,0:T(8,128)(2,1)}, u32[]{:S(2)}) copy-start(bf16[8,80,1280]{2,1,0:T(8,128)(2,1)} %copy-done.6) | copy-start | bytes 4915204
  110.2 31.6 %all-to-all-start.1 = ((bf16[16,80,320]{2,1,0:T(8,128)(2,1)}), bf16[16,80,320]{2,1,0:T(8,128)(2,1)}, u32[]{:S(2)}, u32[]{:S(2)}) async-start(bf16[16,80,320]{2,1,0:T(8,128)(2,1)} %bitcast.24), calls=%async_computation.1 | async-start | bytes 1966080 | tf_op jit(solution)/shard_map/all_to_all | solution.py:375
  116.4 24.2 %collective-permute-start.5 = (bf16[2,8,80,320]{3,2,1,0:T(8,128)(2,1)}, bf16[2,8,80,320]{3,2,1,0:T(8,128)(2,1)S(1)}, u32[]{:S(2)}, u32[]{:S(2)}) collective-permute-start(bf16[2,8,80,320]{3,2,1,0:T(8,128)(2,1)} %fusion.53), channel_id=1, source_target_pairs={{0,1},{1,0},{2,3},{3,2},{4,5},{5,4},{6,7},{7,6},{8,9},{9,8},{10,11... | collective-permute-start | bytes 2457608 | tf_op jit(solution)/shard_map/ppermute | solution.py:392
  141.9 5.9 %copy-start.16 = (f32[8]{0:T(128)S(1)}, f32[8]{0:T(128)}, u32[]{:S(2)}) copy-start(f32[8]{0:T(128)} %param.12) | copy-start | bytes 100
  141.9 27.8 %all-to-all-start = ((bf16[16,80,320]{2,1,0:T(8,128)(2,1)}), bf16[16,80,320]{2,1,0:T(8,128)(2,1)S(1)}, u32[]{:S(2)}, u32[]{:S(2)}) async-start(bf16[16,80,320]{2,1,0:T(8,128)(2,1)} %bitcast.20), calls=%async_computation | async-start | bytes 1966080 | tf_op jit(solution)/shard_map/all_to_all | solution.py:375
  169.6 28.4 %all-to-all-start.3 = ((bf16[16,80,320]{2,1,0:T(8,128)(2,1)}), bf16[16,80,320]{2,1,0:T(8,128)(2,1)S(1)}, u32[]{:S(2)}, u32[]{:S(2)}) async-start(bf16[16,80,320]{2,1,0:T(8,128)(2,1)} %bitcast.31), calls=%async_computation.3 | async-start | bytes 1966080 | tf_op jit(solution)/shard_map/all_to_all | solution.py:403
  198.0 31.6 %all-to-all-start.5 = ((bf16[16,80,320]{2,1,0:T(8,128)(2,1)}), bf16[16,80,320]{2,1,0:T(8,128)(2,1)S(1)}, u32[]{:S(2)}, u32[]{:S(2)}) async-start(bf16[16,80,320]{2,1,0:T(8,128)(2,1)} %bitcast.33), calls=%async_computation.5 | async-start | bytes 1966080 | tf_op jit(solution)/shard_map/all_to_all | solution.py:403
  204.6 24.1 %collective-permute-start.6 = (bf16[16,80,320]{2,1,0:T(8,128)(2,1)S(1)}, bf16[16,80,320]{2,1,0:T(8,128)(2,1)S(1)}, u32[]{:S(2)}, u32[]{:S(2)}) collective-permute-start(bf16[16,80,320]{2,1,0:T(8,128)(2,1)S(1)} %all-to-all-done.3.rows_ref), channel_id=1, source_target_pairs={{0,1},{1,0},{2,3},{3,2},{4,5},{5,4},{6,7},{7,6},{8,9},{9,8},{10,11... | collective-permute-start | bytes 2457608 | tf_op jit(solution)/shard_map/ppermute | solution.py:406
  229.6 27.6 %all-to-all-start.4 = ((bf16[16,80,320]{2,1,0:T(8,128)(2,1)}), bf16[16,80,320]{2,1,0:T(8,128)(2,1)S(1)}, u32[]{:S(2)}, u32[]{:S(2)}) async-start(bf16[16,80,320]{2,1,0:T(8,128)(2,1)} %bitcast.117), calls=%async_computation.4 | async-start | bytes 1966080 | tf_op jit(solution)/shard_map/all_to_all | solution.py:403
  235.4 24.2 %collective-permute-start.7 = (bf16[16,80,320]{2,1,0:T(8,128)(2,1)S(1)}, bf16[16,80,320]{2,1,0:T(8,128)(2,1)}, u32[]{:S(2)}, u32[]{:S(2)}) collective-permute-start(bf16[16,80,320]{2,1,0:T(8,128)(2,1)S(1)} %all-to-all-done.5.rows_ref), channel_id=1, source_target_pairs={{0,1},{1,0},{2,3},{3,2},{4,5},{5,4},{6,7},{7,6},{8,9},{9,8},{10,11... | collective-permute-start | bytes 2457608 | tf_op jit(solution)/shard_map/ppermute | solution.py:406
  257.2 5.9 %copy-start.1 = (bf16[16,80,320]{2,1,0:T(8,128)(2,1)S(1)}, bf16[16,80,320]{2,1,0:T(8,128)(2,1)}, u32[]{:S(2)}) copy-start(bf16[16,80,320]{2,1,0:T(8,128)(2,1)} %copy-done) | copy-start | bytes 2457604
  259.5 23.2 %collective-permute-start.8 = (bf16[16,80,320]{2,1,0:T(8,128)(2,1)S(1)}, bf16[16,80,320]{2,1,0:T(8,128)(2,1)S(1)}, u32[]{:S(2)}, u32[]{:S(2)}) collective-permute-start(bf16[16,80,320]{2,1,0:T(8,128)(2,1)S(1)} %all-to-all-done.4.rows_ref), channel_id=1, source_target_pairs={{0,1},{1,0},{2,3},{3,2},{4,5},{5,4},{6,7},{7,6},{8,9},{9,8},{10,11... | collective-permute-start | bytes 2457608 | tf_op jit(solution)/shard_map/ppermute | solution.py:406
  (12 other events, 26.6 us)
